TPU v7x, 128 devices: a whole 4x4x4 slice. The times are simulated.
128 devices in a mesh: seq: 4 (over y_lo, core), blk: 32 (over x, y_hi, z).
Axes of the slice: x: 4, y: 4 (y_hi: 2, y_lo: 2; y = y_hi * 2 + y_lo), z: 4, core: 2. Of those that a mesh axis runs over, the one named last changes fastest.
Arguments:
- tokens: bfloat16 [32768, 8192], P(('seq', 'blk')), may hold values from -21 to 21
- query_weight: bfloat16 [8192, 1024], replicated, may hold values from -0.0625 to 0.0625
- key_weight: bfloat16 [8192, 128], replicated, may hold values from -0.0625 to 0.0625
- value_weight: bfloat16 [8192, 128], replicated, may hold values from -0.0625 to 0.0625
- doc_lengths: int32 [4, 4], replicated, may hold values from 1 to 4096, 8192 in all within a row
- slot_index: int32 [32768], P(('seq', 'blk')), may hold values from 0 to 32767, as said below
Outputs:
- attended: bfloat16 [32768, 1024], P(('seq', 'blk'))
Inputs may be any that keep to these rules, and one draw needn't show every extreme that they name: `slot_index`: each value appears exactly once. The 256 rows of one loader device put at most 3 rows into the 256 consecutive slots k * 256 to (k + 1) * 256 - 1 of any k, and exactly 3 into some of them.
All inputs are finite; a program needn't handle non-finite values.
Results may differ from a plain program's by a relative error of at most 0.0085.
The roundings to bfloat16 on the way count: a program that leaves them out, or rounds other values in their place, can miss the bound.
Values may be sent and summed in bfloat16 or wider, within the bound.
A program may use at most 128 MiB of HBM per device.

v0:
```python
import math

import jax
import jax.numpy as jnp
from jax import lax
from jax.sharding import PartitionSpec as P

HQ = 8
HS = 128


def rotate_pairs(values, positions):
    half_width = values.shape[-1] // 2
    frequency = 500000.0 ** (-(jnp.arange(half_width, dtype=jnp.float32) * 2.0 / values.shape[-1]))
    angles = positions.astype(jnp.float32)[:, None, None] * frequency[None, None, :]
    cosine = jnp.cos(angles)
    sine_values = jnp.sin(angles)
    leading = values[..., :half_width]
    trailing = values[..., half_width:]
    return jnp.concatenate(
        [leading * cosine - trailing * sine_values, trailing * cosine + leading * sine_values],
        axis=-1,
    )


def doc_positions(lengths_table, local_slot):
    doc_ends = jnp.cumsum(lengths_table, axis=-1)
    starts = doc_ends - lengths_table
    document = jnp.sum((local_slot[:, None] >= doc_ends).astype(jnp.int32), axis=1)
    picked = jnp.arange(lengths_table.shape[-1], dtype=jnp.int32)[None, :] == document[:, None]
    start_of = jnp.sum(jnp.where(picked, starts, 0), axis=1)
    return (document, local_slot - start_of)


def place_slot(local_slot, rows_dev):
    return (local_slot // rows_dev, local_slot % rows_dev)


def slot_of(device, row_index, rows_dev):
    return device * rows_dev + row_index


def project_rows(rows, query_weight, key_weight, value_weight):
    lead_shape = rows.shape[:-1]
    flat_rows = rows.reshape(-1, rows.shape[-1])
    results = []
    for weight in (query_weight, key_weight, value_weight):
        product = jnp.dot(flat_rows, weight, preferred_element_type=jnp.float32)
        results.append(product.reshape(lead_shape + (weight.shape[1],)))
    return (results[0], results[1], results[2])


def finish_rows(query_f, key_f, value_f, positions):
    row_count = query_f.shape[0]
    query_rows = (
        rotate_pairs(query_f.reshape(row_count, HQ, HS), positions)
        .reshape(row_count, HQ * HS)
        .astype(jnp.bfloat16)
    )
    key_rows = rotate_pairs(key_f[:, None, :], positions)[:, 0, :].astype(jnp.bfloat16)
    return (query_rows, key_rows, value_f.astype(jnp.bfloat16))


def arrange_rows(values, where_flat, rows_dev):
    width = values.shape[-1]
    empty = jnp.zeros((rows_dev, width), values.dtype)
    return empty.at[where_flat].set(values.reshape(-1, width), mode="drop")


def shards(tokens, query_weight, key_weight, value_weight, doc_lengths, slot_index):
    rows_dev = tokens.shape[0]
    device_count = lax.axis_size(("seq", "blk"))
    block_count = lax.axis_size("blk")
    group_rows = block_count * rows_dev
    capacity = rows_dev // device_count + 1
    seq_position = lax.axis_index("seq")
    block_position = lax.axis_index("blk")
    seq_count = doc_lengths.shape[0]
    group_of = slot_index // group_rows
    local_of = slot_index % group_rows
    target_block, target_row = place_slot(local_of, rows_dev)
    target = group_of * block_count + target_block
    same_target = target[:, None] == target[None, :]
    row_order = jnp.arange(rows_dev, dtype=jnp.int32)
    earlier = row_order[None, :] < row_order[:, None]
    rank = jnp.sum((same_target & earlier).astype(jnp.int32), axis=1)
    flat_index = target * capacity + rank
    where_send = (
        jnp.full((device_count * capacity,), rows_dev, jnp.int32).at[flat_index].set(target_row)
    )
    where_send = where_send.reshape(device_count, capacity)
    my_local = slot_of(block_position, row_order, rows_dev)
    group_pick = jnp.arange(seq_count, dtype=jnp.int32)[:, None] == seq_position
    my_lengths = jnp.sum(jnp.where(group_pick, doc_lengths, 0), axis=0)[None, :]
    my_doc, my_pos = doc_positions(my_lengths, my_local)
    outgoing = (
        jnp.zeros((device_count * capacity, tokens.shape[1]), jnp.bfloat16)
        .at[flat_index]
        .set(tokens)
    )
    outgoing = outgoing.reshape(device_count, capacity, tokens.shape[1])
    rows_in = lax.all_to_all(outgoing, ("seq", "blk"), split_axis=0, concat_axis=0, tiled=True)
    where_in = lax.all_to_all(where_send, ("seq", "blk"), split_axis=0, concat_axis=0, tiled=True)
    query_f, key_f, value_f = project_rows(rows_in, query_weight, key_weight, value_weight)
    query_f, key_f, value_f, where_recv = (query_f, key_f, value_f, where_in)
    where_flat = where_recv.reshape(-1)
    query_rows, key_rows, value_rows = finish_rows(
        arrange_rows(query_f, where_flat, rows_dev),
        arrange_rows(key_f, where_flat, rows_dev),
        arrange_rows(value_f, where_flat, rows_dev),
        my_pos,
    )
    query_three = query_rows.reshape(rows_dev, HQ, HS)
    score_scale = 1.0 / math.sqrt(HS)
    initial = (
        jnp.full((rows_dev, HQ), -1e30, jnp.float32),
        jnp.zeros((rows_dev, HQ), jnp.float32),
        jnp.zeros((rows_dev, HQ, HS), jnp.float32),
    )
    key_piece = lax.all_gather(key_rows, "blk", axis=0, tiled=True)
    value_piece = lax.all_gather(value_rows, "blk", axis=0, tiled=True)
    key_count = key_piece.shape[0]
    block_width = math.gcd(key_count, 512)
    gathered_rows = jnp.arange(key_count, dtype=jnp.int32)
    key_local = slot_of(gathered_rows // rows_dev, gathered_rows % rows_dev, rows_dev)
    key_doc, unused_pos = doc_positions(my_lengths, key_local)

    def one_block(block_number, running):
        offset = block_number * block_width
        key_block = lax.dynamic_slice_in_dim(key_piece, offset, block_width, 0)
        value_block = lax.dynamic_slice_in_dim(value_piece, offset, block_width, 0)
        local_block = lax.dynamic_slice_in_dim(key_local, offset, block_width, 0)
        doc_block = lax.dynamic_slice_in_dim(key_doc, offset, block_width, 0)
        allowed = (my_doc[:, None] == doc_block[None, :]) & (
            local_block[None, :] <= my_local[:, None]
        )

        def update(current):
            running_max, denominator, numerator = current
            scores = (
                jnp.einsum(
                    "qhd,kd->qhk", query_three, key_block, preferred_element_type=jnp.float32
                )
                * score_scale
            )
            allowed_three = allowed[:, None, :]
            scores = jnp.where(allowed_three, scores, -1e30)
            new_max = jnp.maximum(running_max, jnp.max(scores, axis=-1))
            weights = jnp.where(allowed_three, jnp.exp(scores - new_max[..., None]), 0.0)
            factor = jnp.exp(running_max - new_max)
            denominator = denominator * factor + jnp.sum(weights, axis=-1)
            numerator = numerator * factor[..., None] + jnp.einsum(
                "qhk,kd->qhd",
                weights.astype(jnp.bfloat16),
                value_block,
                preferred_element_type=jnp.float32,
            )
            return (new_max, denominator, numerator)

        def unchanged(current):
            return current

        return lax.cond(jnp.any(allowed), update, unchanged, running)

    final_max, denominator, numerator = lax.fori_loop(
        0, key_count // block_width, one_block, initial
    )
    attended_rows = (
        (numerator / denominator[..., None]).reshape(rows_dev, HQ * HS).astype(jnp.bfloat16)
    )
    is_filled = (where_flat < rows_dev).astype(jnp.bfloat16)
    returning = (
        jnp.take(attended_rows, jnp.minimum(where_flat, rows_dev - 1), axis=0) * is_filled[:, None]
    )
    returning = returning.reshape(device_count, capacity, HQ * HS)
    returned = lax.all_to_all(returning, ("seq", "blk"), split_axis=0, concat_axis=0, tiled=True)
    return jnp.take(returned.reshape(-1, HQ * HS), flat_index, axis=0)


def solution(mesh):
    in_specs = (P(("seq", "blk"), None), P(), P(), P(), P(), P(("seq", "blk")))
    out_specs = P(("seq", "blk"), None)
    return jax.shard_map(shards, mesh=mesh, in_specs=in_specs, out_specs=out_specs, check_vma=False)
```

profile of v0, /device:TPU:1, one launch (start us, length us, event | category | flops | bytes accessed | tf_op | source)
XLA Modules:
  0.0 446.0 jit_solution(17842980668918397970)
XLA Ops:
  6.5 0.8 and_select_fusion
  7.4 0.7 fusion.50
  8.1 0.2 convert_reduce_fusion
  8.3 1.4 scatter_custom_fusion
  9.7 0.8 all_to_all.12
  10.5 11.5 %all-to-all-start = ((s32[128,1,3]{2,1,0:T(1,128)}), s32[128,1,3]{2,1,0:T(1,128)S(1)}, u32[]{:S(2)}, u32[]{:S(2)}) async-start(s32[128,1,3]{2,1,0:T(1,128)} %bitcast.3), calls=%async_computation | async-start | bytes 131072 | tf_op jit(solution)/shard_map/all_to_all | solution.py:103
  22.0 11.3 %scatter_custom_fusion.1 = bf16[384,8192]{1,0:T(8,128)(2,1)} fusion(s32[256]{0:T(256)S(1)} %get-tuple-element.406, bf16[256,8192]{1,0:T(8,128)(2,1)} %param.10, bf16[]{:T(256)} %constant.190.clone.1), kind=kCustom, calls=%fused_computation.30 | custom fusion | bytes 6291968 | tf_op jit(solution)/shard_map/scatter | solution.py:99
  33.3 12.8 %reshape.294 = bf16[128,3,8192]{2,1,0:T(4,128)(2,1)} reshape(bf16[384,8192]{1,0:T(8,128)(2,1)} %scatter_custom_fusion.1) | data formatting | bytes 12582912 | tf_op jit(solution)/shard_map/reshape | solution.py:101
  46.1 10.2 %all-to-all-start.1 = ((bf16[128,3,8192]{2,1,0:T(4,128)(2,1)}), bf16[128,3,8192]{2,1,0:T(4,128)(2,1)}, u32[]{:S(2)}, u32[]{:S(2)}) async-start(bf16[128,3,8192]{2,1,0:T(4,128)(2,1)} %reshape.294), calls=%async_computation.1 | async-start | bytes 16777216 | tf_op jit(solution)/shard_map/all_to_all | solution.py:102
  56.3 0.2 all-gather.6.cloned.1.call-start
  56.7 0.2 reduce-window.6
  57.1 0.5 broadcast.355
  57.6 0.8 broadcast_minimum_fusion
  58.4 0.2 reshape.293
  58.7 105.3 %all-to-all-done.1 = bf16[128,3,8192]{2,1,0:T(4,128)(2,1)} async-done(((bf16[128,3,8192]{2,1,0:T(4,128)(2,1)}), bf16[128,3,8192]{2,1,0:T(4,128)(2,1)}, u32[]{:S(2)}, u32[]{:S(2)}) %all-to-all-start.1) | async-done | bytes 6291488 | tf_op jit(solution)/shard_map/all_to_all | solution.py:102
  164.0 13.8 %reshape.295 = bf16[384,8192]{1,0:T(8,128)(2,1)} reshape(bf16[128,3,8192]{2,1,0:T(4,128)(2,1)} %all-to-all-done.1) | data formatting | bytes 12582912 | tf_op jit(solution)/shard_map/reshape | solution.py:45
  177.8 4.6 %fusion.54 = f32[384,128]{1,0:T(8,128)S(1)} fusion(bf16[384,8192]{1,0:T(8,128)(2,1)} %reshape.295, bf16[8192,128]{1,0:T(8,128)(2,1)S(1)} %copy-done), kind=kOutput, calls=%fused_computation.115 | convolution fusion | flops 805306368 | bytes 8585216 | tf_op jit(solution)/shard_map/dot_general | solution.py:48
  182.3 1.5 scatter_custom_fusion.2
  183.9 0.3 fusion.32
  184.2 0.6 pad_maximum_fusion.1
  184.9 5.2 %fusion.56 = f32[384,128]{1,0:T(8,128)S(1)} fusion(bf16[384,8192]{1,0:T(8,128)(2,1)} %reshape.295, bf16[8192,128]{1,0:T(8,128)(2,1)} %param.13), kind=kOutput, calls=%fused_computation.117 | convolution fusion | flops 805306368 | bytes 8585216 | tf_op jit(solution)/shard_map/dot_general | solution.py:48
  190.1 1.5 scatter_custom_fusion.4
  191.6 0.6 convert_element_type.59
  192.3 0.2 convert_reduce_fusion.1
  192.4 0.3 multiply_cosine_fusion
  192.8 0.1 copy.56
  193.0 13.1 %fusion.55 = f32[384,1024]{1,0:T(8,128)} fusion(bf16[384,8192]{1,0:T(8,128)(2,1)} %reshape.295, bf16[8192,1024]{1,0:T(8,128)(2,1)} %param.11), kind=kOutput, calls=%fused_computation.116 | convolution fusion | flops 6442450944 | bytes 24641536 | tf_op jit(solution)/shard_map/dot_general | solution.py:48
  206.1 3.2 scatter_custom_fusion.3
  209.3 0.3 copy.49
  209.6 0.1 subtract_convert_fusion
  209.8 0.3 copy.51
  210.1 47.2 %all-gather.6.cloned.1.call-done = bf16[8192,1,128]{0,2,1:T(8,128)(2,1)} async-done(((bf16[256,1,128]{0,2,1:T(8,128)(2,1)}), bf16[8192,1,128]{0,2,1:T(8,128)(2,1)}) %all-gather.6.cloned.1.call-update) | async-done | bytes 2097168 | tf_op jit(solution)/shard_map/all_gather | solution.py:120
  257.3 4.1 copy.50
  261.4 69.5 %all-gather.4.cloned.1.call-done = bf16[8192,128]{1,0:T(8,128)(2,1)} async-done(((bf16[256,128]{1,0:T(8,128)(2,1)}), bf16[8192,128]{1,0:T(8,128)(2,1)}) %all-gather.4.cloned.1.call-update) | async-done | bytes 2097168 | tf_op jit(solution)/shard_map/all_gather | solution.py:121
  331.0 32.0 %while.18 = (s32[]{:T(128)}, f32[256,8]{0,1:T(8,128)S(1)}, f32[256,8]{0,1:T(8,128)S(1)}, f32[256,8,128]{2,0,1:T(8,128)S(1)}, s32[256]{0:T(256)S(1)}, /*index=5*/...) while((s32[]{:T(128)}, f32[256,8]{0,1:T(8,128)S(1)}, ...), condition=%wide.region_17.18_spmd.clone, body=%wide.region_11.17_spmd.clone.sunk | while | flops 551555328 | bytes 16138565 | solution.py:165
  331.1 0.8 fusion.66
  332.6 5.3 %conditional.3 = ((f32[256,8]{0,1:T(8,128)S(1)}, f32[256,8]{0,1:T(8,128)S(1)}, f32[256,8,128]{2,0,1:T(8,128)S(1)})) conditional(s32[]{:T(128)} %convert_element_type.80, (f32[256,8]{0,1:T(8,128)S(1)}, f32[256,8]{0,1:T(8,128)S(1)}, f32[256,8,128]{2,0,1:T(8,128)S(1)}) %tuple.65, (pred[256,512]{0,1:T(8,128)(4,1)S(1)}, bf16[8192,128]{1,0:T(8,128)(2,1)}, ...), branch_computations={%region_13.13_spmd, %region_14.16_spmd} | conditional | flops 551030784 | bytes 15991840 | solution.py:163
  332.6 1.7 fusion.2
  334.3 1.0 fusion.4
  335.4 2.5 fusion.8
  338.1 0.8 fusion.66
  339.8 0.8 fusion.66
  341.4 0.8 fusion.66
  343.1 0.8 fusion.66
  344.8 0.8 fusion.66
  346.4 0.8 fusion.66
  348.1 0.8 fusion.66
  349.8 0.8 fusion.66
  351.4 0.8 fusion.66
  353.1 0.8 fusion.66
  354.8 0.8 fusion.66
  356.5 0.8 fusion.66
  358.1 0.8 fusion.66
  359.8 0.8 fusion.66
  361.5 0.8 fusion.66
  363.0 0.3 copy_bitcast_fusion
  363.3 2.1 gather_fusion
  365.4 0.5 gather.11
  365.9 1.7 select_multiply_fusion
  367.7 48.4 %all-to-all-start.2 = ((bf16[128,3,1024]{2,1,0:T(4,128)(2,1)}), bf16[128,3,1024]{2,1,0:T(4,128)(2,1)}, u32[]{:S(2)}, u32[]{:S(2)}) async-start(bf16[128,3,1024]{2,1,0:T(4,128)(2,1)} %select_multiply_fusion), calls=%async_computation.2 | async-start | bytes 2097152 | tf_op jit(solution)/shard_map/all_to_all | solution.py:176
  416.1 18.5 %all-to-all-done.2 = bf16[128,3,1024]{2,1,0:T(4,128)(2,1)} async-done(((bf16[128,3,1024]{2,1,0:T(4,128)(2,1)}), bf16[128,3,1024]{2,1,0:T(4,128)(2,1)}, u32[]{:S(2)}, u32[]{:S(2)}) %all-to-all-start.2) | async-done | bytes 786464 | tf_op jit(solution)/shard_map/all_to_all | solution.py:176
  434.6 2.4 reshape.297
  437.0 1.2 gather_fusion.1
  438.2 0.9 broadcast_select_fusion
  (97 shorter events, 3.5 us)
Async XLA Ops:
  6.5 171.2 %copy-start = (bf16[8192,128]{1,0:T(8,128)(2,1)S(1)}, bf16[8192,128]{1,0:T(8,128)(2,1)}, u32[]{:S(2)}) copy-start(bf16[8192,128]{1,0:T(8,128)(2,1)} %param.12) | copy-start | bytes 6291460
  10.5 35.6 %all-to-all-start = ((s32[128,1,3]{2,1,0:T(1,128)}), s32[128,1,3]{2,1,0:T(1,128)S(1)}, u32[]{:S(2)}, u32[]{:S(2)}) async-start(s32[128,1,3]{2,1,0:T(1,128)} %bitcast.3), calls=%async_computation | async-start | bytes 131072 | tf_op jit(solution)/shard_map/all_to_all | solution.py:103
  46.1 10.5 %copy-start.2 = (s32[4,4]{1,0:T(4,128)S(1)}, s32[4,4]{1,0:T(4,128)}, u32[]{:S(2)}) copy-start(s32[4,4]{1,0:T(4,128)} %param.14) | copy-start | bytes 196
  46.1 117.9 %all-to-all-start.1 = ((bf16[128,3,8192]{2,1,0:T(4,128)(2,1)}), bf16[128,3,8192]{2,1,0:T(4,128)(2,1)}, u32[]{:S(2)}, u32[]{:S(2)}) async-start(bf16[128,3,8192]{2,1,0:T(4,128)(2,1)} %reshape.294), calls=%async_computation.1 | async-start | bytes 16777216 | tf_op jit(solution)/shard_map/all_to_all | solution.py:102
  56.3 201.0 %all-gather.6.cloned.1.call-start = ((), (), s32[]{:S(2)}) async-start(), calls=%async_computation.4 | async-start | bytes 2162688 | tf_op jit(solution)/shard_map/all_gather | solution.py:120
  184.9 146.0 %all-gather.4.cloned.1.call-start = ((), (), s32[]{:S(2)}) async-start(), calls=%async_computation.3 | async-start | bytes 2162688 | tf_op jit(solution)/shard_map/all_gather | solution.py:121
  367.7 67.0 %all-to-all-start.2 = ((bf16[128,3,1024]{2,1,0:T(4,128)(2,1)}), bf16[128,3,1024]{2,1,0:T(4,128)(2,1)}, u32[]{:S(2)}, u32[]{:S(2)}) async-start(bf16[128,3,1024]{2,1,0:T(4,128)(2,1)} %select_multiply_fusion), calls=%async_computation.2 | async-start | bytes 2097152 | tf_op jit(solution)/shard_map/all_to_all | solution.py:176
  416.1 23.0 %copy-start.1 = (bf16[8192,128]{1,0:T(8,128)(2,1)S(1)}, bf16[8192,128]{1,0:T(8,128)(2,1)}, u32[]{:S(2)}) copy-start(bf16[8192,128]{1,0:T(8,128)(2,1)} %param.12) | copy-start | bytes 6291460
Sparse Core Ops, SparseCore 0:
  185.0 72.2 all-gather.5
  260.4 70.3 all-gather.3
where the time goes:
time: 448 us; the launch traced here: 446 us
  waiting for transfers between devices  241 us (54%)
  starting transfers between devices  70.4 us (16%)
  local copies, waits for them, and re-layouts  60.6 us (14%)
  matrix products  27.1 us (6%)
  other arithmetic  23 us (5%)
  between operations  13.7 us (3%)
  loops' own time  10.7 us (2%)
    all_to_all x1, waiting for transfers between devices, shards(): lax.all_to_all(outgoing, ('seq', 'blk'), split_axis=0, concat_axis=0, til...  105 us
    all_gather x1, waiting for transfers between devices, shards(): value_piece = lax.all_gather(value_rows, 'blk', axis=0, tiled=True)  69.5 us
    all_to_all x1, starting transfers between devices, shards(): lax.all_to_all(returning, ('seq', 'blk'), split_axis=0, concat_axis=0, ti...  48.4 us
    all_gather x1, waiting for transfers between devices, shards(): key_piece = lax.all_gather(key_rows, 'blk', axis=0, tiled=True)  47.2 us
    dot_general x3, matrix products, project_rows(): product = jnp.dot(flat_rows, weight, preferred_element_type=jnp.float32)  22.9 us
    all_to_all x1, waiting for transfers between devices, shards(): lax.all_to_all(returning, ('seq', 'blk'), split_axis=0, concat_axis=0, ti...  18.5 us
    reshape x1, local copies, waits for them, and re-layouts, project_rows(): flat_rows = rows.reshape(-1, rows.shape[-1])  13.8 us
    reduce_or x16, other arithmetic, one_block(): return lax.cond(jnp.any(allowed), update, unchanged, running)  13.6 us
  transfers between devices with their start and end apart: 5, of which 4 were waited for; matrix products, arithmetic and copies ran while one was open for 12% of the time, Pallas kernels for 0%

commit v1 on v0

v1 whole, which is shorter than its diff:
```python
import functools
import math

import jax
import jax.numpy as jnp
from jax import lax
from jax.experimental import pallas as pl
from jax.experimental.pallas import tpu as pltpu
from jax.sharding import PartitionSpec as P

HQ = 8
HS = 128
D = 8192
ROWS = 256
NBLOCKS = 32
CAP = 3
PACK = 48
NPACK = 8 * PACK
QW = 128 + HQ * HS
KT = 512
CHUNK = 32
NCHUNK = NPACK // CHUNK
MESH = pl.DeviceIdType.MESH
BF = jnp.bfloat16
F32 = jnp.float32
HIGHEST = lax.Precision.HIGHEST


def place():
    seq = lax.axis_index("seq")
    blk = lax.axis_index("blk")
    core = seq % 2
    y = (blk // 4) % 2 * 2 + seq // 2
    return blk // 8, y, blk % 4, core


def device(x, y, z, c):
    return ((y % 2) * 2 + c, (x * 2 + y // 2) * 4 + z)


def block_id(x, y, c):
    return c * 16 + x * 4 + y


def dot_t(a, b):
    return lax.dot_general(a, b, (((0,), (0,)), ((), ())), preferred_element_type=F32)


def rope(v, cos, sin):
    return v * cos + pltpu.roll(v, HS // 2, 1) * sin


def front_kernel(
    tok, wq, wk, wv, cos, sin, meta, pidx,
    qin, kall, vtall,
    tok_v, wkv_v, wq_v, acc, kvs, zin, perm, aout, ain, kblk, vblk, qs,
    tok_sem, wq_sem, zs_sem, zr_sem, as_sem, ar_sem, qs_sem, qr_sem,
    ts_sem, tr_sem, ds_sem, dr_sem, loc_sem,
):
    x, y, z, c = place()
    kc = D // 4
    mine = block_id(x, y, c)
    line = z * 2 + c

    loads = []
    for i in range(4):
        part = pl.ds(i * kc, kc)
        loads.append([
            pltpu.make_async_copy(tok.at[:, part], tok_v.at[:, part], tok_sem.at[0, i]),
            pltpu.make_async_copy(wk.at[part, :], wkv_v.at[part, pl.ds(0, HS)], tok_sem.at[1, i]),
            pltpu.make_async_copy(wv.at[part, :], wkv_v.at[part, pl.ds(HS, HS)], tok_sem.at[2, i]),
        ])
        for load in loads[i]:
            load.start()
    qloads = []
    for n in range(4):
        cols = pl.ds(n * 256, 256)
        qloads.append(pltpu.make_async_copy(wq.at[:, cols], wq_v.at[n], wq_sem.at[n]))
        qloads[n].start()

    peers = []
    for dz in range(4):
        for dc in range(2):
            if (dz, dc) != (0, 0):
                peers.append(((z + dz) % 4, (c + dc) % 2))
    flat = []
    for dx in range(4):
        for dy in range(4):
            for dc in range(2):
                if (dx, dy, dc) != (0, 0, 0):
                    flat.append(((x + dx) % 4, (y + dy) % 4, (c + dc) % 2))
    barrier = pltpu.get_barrier_semaphore()
    for pz, pc in peers:
        pl.semaphore_signal(barrier, inc=1, device_id=device(x, y, pz, pc), device_id_type=MESH)
    for px, py, pc in flat:
        if True:
            pl.semaphore_signal(barrier, inc=1, device_id=device(px, py, z, pc), device_id_type=MESH)

    lane = lax.broadcasted_iota(jnp.int32, (NPACK, ROWS), 0)
    pack = (lane == pidx[...]).astype(F32).astype(BF)
    row = lax.broadcasted_iota(jnp.int32, (512, NPACK), 0)
    col = lax.broadcasted_iota(jnp.int32, (512, NPACK), 1)
    j = row >> 4
    slot12 = row & 15
    zz = (slot12 >= 3).astype(jnp.int32) + (slot12 >= 6).astype(jnp.int32) + (slot12 >= 9).astype(jnp.int32)
    source = zz * 96 + (j & 1) * 48 + (j >> 1) * 3 + (slot12 - 3 * zz)
    perm[...] = ((source == col) & (slot12 < 12)).astype(F32).astype(BF)

    for i in range(4):
        part = pl.ds(i * kc, kc)
        for load in loads[i]:
            load.wait()
        product = jnp.dot(tok_v[:, part], wkv_v[part, :], preferred_element_type=F32)
        if i == 0:
            acc[...] = product
        else:
            acc[...] += product
    k_rows = rope(acc[:, :HS], cos[...], sin[...]).astype(BF)
    v_rows = acc[:, HS:].astype(BF)
    kvs[:, 0:HS] = jnp.dot(pack, k_rows, preferred_element_type=F32).astype(BF)
    kvs[:, HS:2 * HS] = jnp.dot(pack, v_rows, preferred_element_type=F32).astype(BF)
    slots = jnp.dot(pack, meta[...], preferred_element_type=F32).astype(BF)
    kvs[:, 2 * HS:] = slots
    qs[:, 0:128] = slots

    pl.semaphore_wait(barrier, 7 + 31)

    sends = []
    for dz in range(1, 4):
        pz = (z + dz) % 4
        sends.append(pltpu.make_async_remote_copy(
            src_ref=kvs.at[pl.ds(pz * 96, 96), :], dst_ref=zin.at[pl.ds(z * 96, 96), :],
            send_sem=zs_sem.at[dz - 1], recv_sem=zr_sem.at[0],
            device_id=device(x, y, pz, c), device_id_type=MESH))
        sends[-1].start()
    pltpu.make_async_copy(
        kvs.at[pl.ds(z * 96, 96), :], zin.at[pl.ds(z * 96, 96), :], zr_sem.at[0]).start()

    def query_block(n):
        qloads[n].wait()

        def step(i, total):
            part = pl.ds(pl.multiple_of(i * kc, kc), kc)
            return total + jnp.dot(tok_v[:, part], wq_v[n, part, :], preferred_element_type=F32)

        acc[...] = jnp.zeros_like(acc)

        @pl.loop(0, 4)
        def _(i):
            part = pl.ds(pl.multiple_of(i * kc, kc), kc)
            acc[...] += jnp.dot(tok_v[:, part], wq_v[n, part, :], preferred_element_type=F32)

        for h in range(2):
            rows = rope(acc[:, h * HS:(h + 1) * HS], cos[...], sin[...]).astype(BF)
            at = 128 + (n * 2 + h) * HS
            qs[:, at:at + HS] = jnp.dot(pack, rows, preferred_element_type=F32).astype(BF)

    def query_send(half):
        cols = pl.ds(0, 640) if half == 0 else pl.ds(640, 512)
        for i, (pz, pc) in enumerate(peers):
            sends.append(pltpu.make_async_remote_copy(
                src_ref=qs.at[pl.ds((pz * 2 + pc) * PACK, PACK), cols],
                dst_ref=qin.at[pl.ds(line * PACK, PACK), cols],
                send_sem=qs_sem.at[half, i], recv_sem=qr_sem.at[0],
                device_id=device(x, y, pz, pc), device_id_type=MESH))
            sends[-1].start()
        pltpu.make_async_copy(
            qs.at[pl.ds(line * PACK, PACK), cols], qin.at[pl.ds(line * PACK, PACK), cols],
            qr_sem.at[0]).start()

    query_block(0)

    pltpu.make_async_copy(zin, zin, zr_sem.at[0]).wait()
    aout[...] = jnp.dot(perm[...], zin[...], preferred_element_type=F32).astype(BF)
    for i, (px, py, pc) in enumerate(flat):
        sends.append(pltpu.make_async_remote_copy(
            src_ref=aout.at[pl.ds(block_id(px, py, pc) * 16, 16), :],
            dst_ref=ain.at[pl.ds(mine * 16, 16), :],
            send_sem=as_sem.at[i], recv_sem=ar_sem.at[0],
            device_id=device(px, py, z, pc), device_id_type=MESH))
        sends[-1].start()
    pltpu.make_async_copy(
        aout.at[pl.ds(mine * 16, 16), :], ain.at[pl.ds(mine * 16, 16), :], ar_sem.at[0]).start()

    query_block(1)
    query_send(0)

    pltpu.make_async_copy(ain, ain, ar_sem.at[0]).wait()
    got = ain[:, 2 * HS:].astype(F32)
    want = (lax.broadcasted_iota(jnp.int32, (512, HS), 1) + 1).astype(F32)
    one = jnp.concatenate([
        (got == want).astype(F32), (got == want + 128.0).astype(F32)], axis=1).astype(BF)
    kblk[...] = dot_t(one, ain[:, 0:HS]).astype(BF)
    vblk[...] = dot_t(ain[:, HS:2 * HS], one).astype(BF)

    def where(o):
        return block_id((x + o[0]) % 4, (y + o[1]) % 4, c)

    def piece(q, o):
        if q < 2:
            return kall.at[where(o), pl.ds(q * 128, 128), :]
        return vtall.at[where(o), pl.ds((q - 2) * 64, 64), :]

    def own(q):
        if q < 2:
            return kblk.at[pl.ds(q * 128, 128), :]
        return vblk.at[pl.ds((q - 2) * 64, 64), :]

    count = [0]

    def push(q, o, step):
        e = ((step[0]) % 4, (step[1]) % 4)
        rel = ((o[0] - e[0]) % 4, (o[1] - e[1]) % 4)
        src = own(q) if o == (0, 0) else piece(q, o)
        sends.append(pltpu.make_async_remote_copy(
            src_ref=src, dst_ref=piece(q, o),
            send_sem=ts_sem.at[count[0]], recv_sem=tr_sem.at[q * 16 + rel[0] * 4 + rel[1]],
            device_id=device((x + e[0]) % 4, (y + e[1]) % 4, z, c), device_id_type=MESH))
        sends[-1].start()
        count[0] += 1

    def share(q, o):
        src = own(q) if o == (0, 0) else piece(q, o)
        sends.append(pltpu.make_async_remote_copy(
            src_ref=src, dst_ref=piece(q, o),
            send_sem=ds_sem.at[q * 16 + o[0] * 4 + o[1]], recv_sem=dr_sem.at[0 if q < 2 else 1],
            device_id=device(x, y, z, 1 - c), device_id_type=MESH))
        sends[-1].start()

    def axes(q):
        return ((1, 0), (0, 1)) if q < 2 else ((0, 1), (1, 0))

    def offset(q, a, b):
        first, second = axes(q)
        return ((a * first[0] + b * second[0]) % 4, (a * first[1] + b * second[1]) % 4)

    def scaled(v, d):
        return (v[0] * d, v[1] * d)

    def forward(q, a, b):
        first, second = axes(q)
        d = 1 if q % 2 == 0 else -1
        o = offset(q, a, b)
        if b == 0:
            if a == 0:
                push(q, o, scaled(first, 1))
                push(q, o, scaled(first, -1))
            elif a == (-d) % 4:
                push(q, o, scaled(first, d))
            push(q, o, scaled(second, 1))
            push(q, o, scaled(second, -1))
        elif b == (-d) % 4:
            push(q, o, scaled(second, d))
        share(q, o)

    local = []
    for q in range(4):
        local.append(pltpu.make_async_copy(own(q), piece(q, (0, 0)), loc_sem.at[q]))
        local[-1].start()
        forward(q, 0, 0)

    query_block(2)

    def arrive(q, a, b):
        o = offset(q, a, b)
        ref = piece(q, o)
        pltpu.make_async_copy(ref, ref, tr_sem.at[q * 16 + o[0] * 4 + o[1]]).wait()
        forward(q, a, b)

    for a, b in ((1, 0), (3, 0), (0, 1), (0, 3)):
        for q in range(4):
            arrive(q, a, b)

    query_block(3)
    query_send(1)

    for a, b in ((2, 0), (1, 1), (1, 3), (3, 1), (3, 3), (0, 2), (2, 1), (2, 3), (1, 2), (3, 2), (2, 2)):
        for q in range(4):
            arrive(q, a, b)

    other = pl.ds((1 - c) * 16, 16)
    pltpu.make_async_copy(kall.at[other], kall.at[other], dr_sem.at[0]).wait()
    pltpu.make_async_copy(vtall.at[other], vtall.at[other], dr_sem.at[1]).wait()
    pltpu.make_async_copy(qin, qin, qr_sem.at[0]).wait()
    for copy in local:
        copy.wait()
    for copy in sends:
        copy.wait_send()


def front(tokens, wq, wk, wv, cos, sin, meta, pidx):
    anyspace = pl.BlockSpec(memory_space=pl.ANY)
    vmem = pl.BlockSpec(memory_space=pltpu.VMEM)
    dma = pltpu.SemaphoreType.DMA
    return pl.pallas_call(
        front_kernel,
        out_shape=(
            jax.ShapeDtypeStruct((NPACK, QW), BF),
            jax.ShapeDtypeStruct((NBLOCKS, ROWS, HS), BF),
            jax.ShapeDtypeStruct((NBLOCKS, HS, ROWS), BF),
        ),
        in_specs=[anyspace] * 4 + [vmem] * 4,
        out_specs=(anyspace, anyspace, anyspace),
        scratch_shapes=[
            pltpu.VMEM((ROWS, D), BF),
            pltpu.VMEM((D, 2 * HS), BF),
            pltpu.VMEM((4, D, 256), BF),
            pltpu.VMEM((ROWS, 256), F32),
            pltpu.VMEM((NPACK, 3 * HS), BF),
            pltpu.VMEM((NPACK, 3 * HS), BF),
            pltpu.VMEM((512, NPACK), BF),
            pltpu.VMEM((512, 3 * HS), BF),
            pltpu.VMEM((512, 3 * HS), BF),
            pltpu.VMEM((ROWS, HS), BF),
            pltpu.VMEM((HS, ROWS), BF),
            pltpu.VMEM((NPACK, QW), BF),
            dma((3, 4)), dma((4,)), dma((3,)), dma((1,)), dma((31,)), dma((1,)),
            dma((2, 7)), dma((1,)), dma((60,)), dma((64,)), dma((64,)), dma((2,)), dma((4,)),
        ],
        compiler_params=pltpu.CompilerParams(
            collective_id=0, has_side_effects=True, vmem_limit_bytes=50 << 20),
        name="front",
    )(tokens, wq, wk, wv, cos, sin, meta, pidx)


def attend_kernel(ends, qin, kall, vtall, out, rank_s, slot_s, one_s, qsort, osort):
    c = ends[4]
    shape = (NPACK, HS)
    i = lax.broadcasted_iota(jnp.int32, shape, 0)
    w = i - ((i * 43691) >> 21) * PACK
    base = ((w * 43691) >> 17) * 2 + c
    m = qin[:, 0:HS].astype(F32)
    slot = jnp.where(m > 0.0, base.astype(F32) * 256.0 + m - 1.0, 8192.0 + i.astype(F32))
    slot_row = jnp.transpose(slot)[0:1, :]
    slot_wide = jnp.concatenate([slot] * 3, axis=1)
    rank = jnp.sum((slot_row < slot_wide).astype(F32), axis=1, keepdims=True)
    lane = lax.broadcasted_iota(jnp.int32, (NPACK, NPACK), 1).astype(F32)
    one = (lane == rank).astype(F32)
    one_s[...] = one.astype(BF)
    rank_s[...] = jnp.broadcast_to(rank, shape)
    slot_s[...] = slot
    qsort[...] = dot_t(one_s[...], qin[:, HS:]).astype(BF)
    osort[...] = jnp.zeros_like(osort)
    scale = math.log2(math.e) / math.sqrt(HS)
    wide = CHUNK * HQ

    def chunk(n, carry):
        lane_q = (lax.broadcasted_iota(jnp.int32, (NPACK, HS), 1) & (CHUNK - 1)) + n * CHUNK
        pick = rank_s[...] == lane_q.astype(F32)
        half = jnp.sum(jnp.where(pick, slot_s[...], 0.0), axis=0, keepdims=True)
        mine = jnp.concatenate([half, half], axis=1).astype(jnp.int32)
        start = jnp.zeros_like(mine)
        for d in range(3):
            start = jnp.where(mine >= ends[d], ends[d], start)
        low = jnp.min(start)
        high = jnp.max(jnp.where(mine < 8192, mine, -1))

        @pl.when(high >= 0)
        def _():
            rows = pl.ds(pl.multiple_of(n * CHUNK, CHUNK), CHUNK)
            queries = jnp.concatenate(
                [qsort[rows, h * HS:(h + 1) * HS] for h in range(HQ)], axis=0)

            def tile(t, state):
                top, total, acc = state
                keys = kall[pl.ds(pl.multiple_of(t * KT, KT), KT), :]
                s = lax.dot_general(keys, queries, (((1,), (1,)), ((), ())), preferred_element_type=F32)
                at = lax.broadcasted_iota(jnp.int32, (KT, wide), 0) + t * KT
                allowed = (at >= start) & (at <= mine)
                s = jnp.where(allowed, s, -1e30)
                new = jnp.maximum(top, jnp.max(s, axis=0, keepdims=True))
                p = jnp.exp2((s - new) * scale)
                factor = jnp.exp2((top - new) * scale)
                total = total * factor + jnp.sum(p, axis=0, keepdims=True)
                pb = p.astype(BF)
                acc = acc * factor
                for u in range(KT // ROWS):
                    acc = acc + jnp.dot(
                        vtall[t * (KT // ROWS) + u], pb[u * ROWS:(u + 1) * ROWS, :],
                        preferred_element_type=F32)
                return new, total, acc

            state = (
                jnp.full((1, wide), -1e30, F32), jnp.zeros((1, wide), F32), jnp.zeros((HS, wide), F32))
            top, total, acc = lax.fori_loop(low // KT, high // KT + 1, tile, state)
            o = jnp.transpose(acc / total).astype(BF)
            for h in range(HQ):
                osort[rows, h * HS:(h + 1) * HS] = o[h * CHUNK:(h + 1) * CHUNK, :]

        return carry

    lax.fori_loop(0, NCHUNK, chunk, 0)
    out[...] = jnp.dot(one_s[...], osort[...], preferred_element_type=F32).astype(BF)


def attend(ends, qin, kall, vtall):
    vmem = pl.BlockSpec(memory_space=pltpu.VMEM)
    return pl.pallas_call(
        attend_kernel,
        out_shape=jax.ShapeDtypeStruct((NPACK, HQ * HS), BF),
        in_specs=[pl.BlockSpec(memory_space=pltpu.SMEM), vmem, vmem, vmem],
        out_specs=vmem,
        scratch_shapes=[
            pltpu.VMEM((NPACK, HS), F32),
            pltpu.VMEM((NPACK, HS), F32),
            pltpu.VMEM((NPACK, NPACK), BF),
            pltpu.VMEM((NPACK, HQ * HS), BF),
            pltpu.VMEM((NPACK, HQ * HS), BF),
        ],
        compiler_params=pltpu.CompilerParams(vmem_limit_bytes=40 << 20),
        name="attend",
    )(ends, qin, kall.reshape(NBLOCKS * ROWS, HS), vtall)


def back_kernel(packed, ret, send_sem, recv_sem):
    x, y, z, c = place()
    line = z * 2 + c
    peers = []
    for dz in range(4):
        for dc in range(2):
            if (dz, dc) != (0, 0):
                peers.append(((z + dz) % 4, (c + dc) % 2))
    barrier = pltpu.get_barrier_semaphore()
    for pz, pc in peers:
        pl.semaphore_signal(barrier, inc=1, device_id=device(x, y, pz, pc), device_id_type=MESH)
    pl.semaphore_wait(barrier, 7)
    sends = []
    for i, (pz, pc) in enumerate(peers):
        sends.append(pltpu.make_async_remote_copy(
            src_ref=packed.at[pl.ds((pz * 2 + pc) * PACK, PACK), :],
            dst_ref=ret.at[pl.ds(line * PACK, PACK), :],
            send_sem=send_sem.at[i], recv_sem=recv_sem.at[0],
            device_id=device(x, y, pz, pc), device_id_type=MESH))
        sends[-1].start()
    pltpu.make_async_copy(
        packed.at[pl.ds(line * PACK, PACK), :], ret.at[pl.ds(line * PACK, PACK), :], recv_sem.at[0]).start()
    pltpu.make_async_copy(ret, ret, recv_sem.at[0]).wait()
    for copy in sends:
        copy.wait_send()


def back(packed):
    anyspace = pl.BlockSpec(memory_space=pl.ANY)
    return pl.pallas_call(
        back_kernel,
        out_shape=jax.ShapeDtypeStruct((NPACK, HQ * HS), BF),
        in_specs=[anyspace],
        out_specs=anyspace,
        scratch_shapes=[pltpu.SemaphoreType.DMA((7,)), pltpu.SemaphoreType.DMA((1,))],
        compiler_params=pltpu.CompilerParams(collective_id=1, has_side_effects=True),
        name="back",
    )(packed)


def shards(tokens, query_weight, key_weight, value_weight, doc_lengths, slot_index):
    x, y, z, c = place()
    order = jnp.arange(ROWS, dtype=jnp.int32)
    block = slot_index // ROWS
    same = block[:, None] == block[None, :]
    rank = jnp.sum((same & (order[None, :] < order[:, None])).astype(jnp.int32), axis=1)
    group = block // NBLOCKS
    local_block = block % NBLOCKS
    pidx = group * 96 + (local_block % 2) * PACK + (local_block // 2) * CAP + rank
    local = slot_index % (NBLOCKS * ROWS)
    ends = jnp.cumsum(doc_lengths, axis=1)
    in_group = group[:, None] == jnp.arange(4, dtype=jnp.int32)[None, :]
    start = jnp.zeros_like(local)
    for d in range(3):
        end = jnp.sum(jnp.where(in_group, ends[:, d][None, :], 0), axis=1)
        start = jnp.where(local >= end, end, start)
    position = local - start
    frequency = 500000.0 ** (-(jnp.arange(HS // 2, dtype=F32) * 2.0 / HS))
    angles = position.astype(F32)[:, None] * frequency[None, :]
    cosine = jnp.cos(angles)
    sine = jnp.sin(angles)
    cos = jnp.concatenate([cosine, cosine], axis=1)
    sin = jnp.concatenate([-sine, sine], axis=1)
    meta = jnp.broadcast_to((slot_index % ROWS + 1).astype(BF)[:, None], (ROWS, HS))
    qin, kall, vtall = front(
        tokens, query_weight, key_weight, value_weight, cos, sin, meta, pidx[None, :])
    mine = jnp.sum(jnp.where(jnp.arange(4)[:, None] == z, ends, 0), axis=0)
    scalars = jnp.concatenate([mine, c[None], jnp.zeros((3,), jnp.int32)]).astype(jnp.int32)
    packed = attend(scalars, qin, kall, vtall)
    returned = back(packed)
    pick = (pidx[:, None] == jnp.arange(NPACK, dtype=jnp.int32)[None, :]).astype(BF)
    return jnp.dot(pick, returned, preferred_element_type=F32).astype(BF)


def solution(mesh):
    in_specs = (P(("seq", "blk"), None), P(), P(), P(), P(), P(("seq", "blk")))
    out_specs = P(("seq", "blk"), None)
    return jax.shard_map(shards, mesh=mesh, in_specs=in_specs, out_specs=out_specs, check_vma=False)
```

time: 448 us -> 100 us (0.22)
  waiting for transfers between devices: 241 us -> 0 us
  Pallas kernels: 0 us -> 91.2 us
  starting transfers between devices: 70.4 us -> 0 us
  local copies, waits for them, and re-layouts: 60.6 us -> 2.73 us
  matrix products: 27.1 us -> 2.42 us
  other arithmetic: 23 us -> 3.39 us
  between operations: 13.7 us -> 0.08 us
  loops' own time: 10.7 us -> 0 us
    all_to_all x3 -> x0, waiting for transfers between devices: 124 us -> none  [the longest x1 105 us: shards(): lax.all_to_all(outgoing, ('seq', 'blk'), split_axis=0, concat_axis=0, til...]
    all_gather x2 -> x0, waiting for transfers between devices: 117 us -> none  [the longest x1 69.5 us: shards(): value_piece = lax.all_gather(value_rows, 'blk', axis=0, tiled=True)]
    pallas_call x0 -> x3, Pallas kernels: none -> 91.2 us  [the longest x1 49.8 us: front(): pl.pallas_call(front_kernel, out_shape=(jax.ShapeDtypeStruct((NPACK, QW),...]
    all_to_all x3 -> x0, starting transfers between devices: 70.1 us -> none  [the longest x1 48.4 us: shards(): lax.all_to_all(returning, ('seq', 'blk'), split_axis=0, concat_axis=0, ti...]
    reshape x4 -> x0, local copies, waits for them, and re-layouts: 29.2 us -> none  [the longest x1 13.8 us: project_rows(): flat_rows = rows.reshape(-1, rows.shape[-1])]
    dot_general x5 -> x1, matrix products: 27.1 us -> 2.42 us  [shards(): return jnp.dot(pick, returned, preferred_element_type=F32).astype(BF)]
    scatter x7 -> x0, local copies, waits for them, and re-layouts: 19.2 us -> none  [the longest x1 11.3 us: shards(): outgoing = jnp.zeros((device_count * capacity, tokens.shape[1]), jnp.bflo...]
    reduce_or x16 -> x0, other arithmetic: 13.6 us -> none  [one_block(): return lax.cond(jnp.any(allowed), update, unchanged, running)]
  transfers between devices with their start and end apart: 5 -> 0, of which waited for: 4 -> 0; matrix products, arithmetic and copies ran while one was open for 12% -> 0% of each run, Pallas kernels for 0% -> 0%
where the time goes in v1:
time: 100 us; the launch traced here: 99.8 us
  Pallas kernels  91.2 us (91%)
  other arithmetic  3.39 us (3%)
  local copies, waits for them, and re-layouts  2.73 us (3%)
  matrix products  2.42 us (2%)
    pallas_call x1, Pallas kernels, front(): pl.pallas_call(front_kernel, out_shape=(jax.ShapeDtypeStruct((NPACK, QW),...  49.8 us
    pallas_call x1, Pallas kernels, attend(): pl.pallas_call(attend_kernel, out_shape=jax.ShapeDtypeStruct((NPACK, HQ *...  24.5 us
    pallas_call x1, Pallas kernels, back(): pl.pallas_call(back_kernel, out_shape=jax.ShapeDtypeStruct((NPACK, HQ * H...  16.8 us
    unnamed x4, local copies, waits for them, and re-layouts  2.45 us
    dot_general x1, matrix products, shards(): return jnp.dot(pick, returned, preferred_element_type=F32).astype(BF)  2.42 us

profile of v1, /device:TPU:1, one launch (start us, length us, event | category | flops | bytes accessed | tf_op | source)
XLA Modules:
  0.0 99.8 jit_solution(4945903165340172559)
XLA Ops:
  0.0 0.7 fusion.10
  0.7 0.2 convert_reduce_fusion
  0.9 0.9 reduce_window_sum.11
  1.8 0.1 select_reduce_fusion.3
  1.9 0.1 pad_add_fusion.ends
  1.9 0.2 slice_reduce_fusion
  2.1 0.1 select_reduce_fusion
  2.2 0.7 fusion.4
  2.9 0.1 broadcast_in_dim.76.meta
  3.0 0.5 fusion.2
  3.6 0.1 pad_maximum_fusion
  3.7 49.8 %front.1 = (bf16[384,1152]{1,0:T(8,128)(2,1)S(1)}, bf16[32,256,128]{2,1,0:T(8,128)(2,1)S(1)}, bf16[32,128,256]{2,1,0:T(8,128)(2,1)}) custom-call(bf16[256,8192]{1,0:T(8,128)(2,1)} %tok.1, bf16[8192,1024]{1,0:T(8,128)(2,1)} %wq.1, bf16[8192,128]{1,0:T(8,128)(2,1)} %wk.1, bf16[8192,128]{1,0:T(8,128)(2,1)} %wv.1, f32[256,128]{1,0:T(8,128)S(1)} %get-tuple-element.24.cos, ...), custom_call_target="tpu_custom_call" | custom-call | tf_op jit(solution)/shard_map/front/pallas_call | solution.py:295
  53.5 0.0 copy-start.1
  53.5 1.6 %copy-done.1 = bf16[32,128,256]{2,1,0:T(8,128)(2,1)S(1)} copy-done((bf16[32,128,256]{2,1,0:T(8,128)(2,1)S(1)}, bf16[32,128,256]{2,1,0:T(8,128)(2,1)}, u32[]{:S(2)}) %copy-start.1) | copy-done | bytes 2097176
  55.1 24.5 %attend.1.packed = bf16[384,1024]{1,0:T(8,128)(2,1)S(1)} custom-call(s32[8]{0:T(128)S(1)} %pad_add_fusion.ends, bf16[384,1152]{1,0:T(8,128)(2,1)S(1)} %get-tuple-element.8.qin, bf16[8192,128]{1,0:T(8,128)(2,1)S(1)} %bitcast.4, bf16[32,128,256]{2,1,0:T(8,128)(2,1)S(1)} %copy-done.1), custom_call_target="tpu_custom_call" | custom-call | tf_op jit(solution)/shard_map/attend/pallas_call | solution.py:398
  79.6 0.0 copy-start
  79.7 0.9 copy-done
  80.5 16.8 %back.1 = bf16[384,1024]{1,0:T(8,128)(2,1)} custom-call(bf16[384,1024]{1,0:T(8,128)(2,1)} %copy-done), custom_call_target="tpu_custom_call" | custom-call | tf_op jit(solution)/shard_map/back/pallas_call | solution.py:444
  97.4 2.4 %convolution_convert_fusion = bf16[256,1024]{1,0:T(8,128)(2,1)} fusion(bf16[384,1024]{1,0:T(8,128)(2,1)} %back.1, s32[256]{0:T(256)S(1)} %get-tuple-element.17), kind=kOutput, calls=%fused_computation | convolution fusion | flops 201687040 | bytes 1311744 | tf_op jit(solution)/shard_map/dot_general | solution.py:486
  (4 shorter events, 0.0 us)
Async XLA Ops:
  53.5 1.6 %copy-start.1 = (bf16[32,128,256]{2,1,0:T(8,128)(2,1)S(1)}, bf16[32,128,256]{2,1,0:T(8,128)(2,1)}, u32[]{:S(2)}) copy-start(bf16[32,128,256]{2,1,0:T(8,128)(2,1)} %get-tuple-element.10.vtall) | copy-start | bytes 6291460
  79.6 0.9 copy-start

commit v2 on v1

v2 whole, which is shorter than its diff:
```python
import functools
import math

import jax
import jax.numpy as jnp
from jax import lax
from jax.experimental import pallas as pl
from jax.experimental.pallas import tpu as pltpu
from jax.sharding import PartitionSpec as P

HQ = 8
HS = 128
D = 8192
ROWS = 256
NBLOCKS = 32
CAP = 3
PACK = 48
NPACK = 8 * PACK
QW = 128 + HQ * HS
KT = 512
KPARTS = 8
CHUNK = 32
NCHUNK = NPACK // CHUNK
MESH = pl.DeviceIdType.MESH
BF = jnp.bfloat16
F32 = jnp.float32
HIGHEST = lax.Precision.HIGHEST


def place():
    seq = lax.axis_index("seq")
    blk = lax.axis_index("blk")
    core = seq % 2
    y = (blk // 4) % 2 * 2 + seq // 2
    return blk // 8, y, blk % 4, core


def device(x, y, z, c):
    return ((y % 2) * 2 + c, (x * 2 + y // 2) * 4 + z)


def block_id(x, y, c):
    return c * 16 + x * 4 + y


def dot_t(a, b):
    return lax.dot_general(a, b, (((0,), (0,)), ((), ())), preferred_element_type=F32)


def rope(v, cos, sin):
    return v * cos + pltpu.roll(v, HS // 2, 1) * sin


def starts(slots, ends):
    start = jnp.zeros_like(slots)
    for d in range(3):
        start = jnp.where(slots >= ends[d], ends[d], start)
    return start


def front_kernel(
    ends, tok, wq, wk, wv, cos, sin, meta, pidx,
    kall, vtall, qsort, one_o, lanes_o, bounds_o,
    tok_v, wkv_v, wq_v, acc, kvs, zin, perm, aout, ain, kblk, vblk, qs, qin,
    tok_sem, wq_sem, zs_sem, zr_sem, as_sem, ar_sem, qs_sem, qr_sem,
    ts_sem, tr_sem, ds_sem, dr_sem, loc_sem,
):
    x, y, z, c = place()
    kc = D // KPARTS
    mine = block_id(x, y, c)
    line = z * 2 + c

    loads = []
    for i in range(KPARTS):
        part = pl.ds(i * kc, kc)
        loads.append([
            pltpu.make_async_copy(tok.at[:, part], tok_v.at[:, part], tok_sem.at[0, i]),
            pltpu.make_async_copy(wk.at[part, :], wkv_v.at[part, pl.ds(0, HS)], tok_sem.at[1, i]),
            pltpu.make_async_copy(wv.at[part, :], wkv_v.at[part, pl.ds(HS, HS)], tok_sem.at[2, i]),
        ])
        for load in loads[i]:
            load.start()
    qloads = []
    for n in range(4):
        cols = pl.ds(n * 256, 256)
        qloads.append(pltpu.make_async_copy(wq.at[:, cols], wq_v.at[n], wq_sem.at[n]))

    peers = []
    for dz in range(4):
        for dc in range(2):
            if (dz, dc) != (0, 0):
                peers.append(((z + dz) % 4, (c + dc) % 2))
    flat = []
    for dx in range(4):
        for dy in range(4):
            for dc in range(2):
                if (dx, dy, dc) != (0, 0, 0):
                    flat.append(((x + dx) % 4, (y + dy) % 4, (c + dc) % 2))
    barrier = pltpu.get_barrier_semaphore()
    for pz, pc in peers:
        pl.semaphore_signal(barrier, inc=1, device_id=device(x, y, pz, pc), device_id_type=MESH)
    for px, py, pc in flat:
        pl.semaphore_signal(barrier, inc=1, device_id=device(px, py, z, pc), device_id_type=MESH)

    lane = lax.broadcasted_iota(jnp.int32, (NPACK, ROWS), 0)
    pack = (lane == pidx[...]).astype(F32).astype(BF)
    row = lax.broadcasted_iota(jnp.int32, (512, NPACK), 0)
    col = lax.broadcasted_iota(jnp.int32, (512, NPACK), 1)
    j = row >> 4
    slot12 = row & 15
    zz = (slot12 >= 3).astype(jnp.int32) + (slot12 >= 6).astype(jnp.int32) + (slot12 >= 9).astype(jnp.int32)
    source = zz * 96 + (j & 1) * 48 + (j >> 1) * 3 + (slot12 - 3 * zz)
    perm[...] = ((source == col) & (slot12 < 12)).astype(F32).astype(BF)
    slots = jnp.dot(pack, meta[...], preferred_element_type=F32).astype(BF)
    kvs[:, 2 * HS:] = slots
    qs[:, 0:128] = slots

    for i in range(KPARTS):
        part = pl.ds(i * kc, kc)
        for load in loads[i]:
            load.wait()
        product = jnp.dot(tok_v[:, part], wkv_v[part, :], preferred_element_type=F32)
        if i == 0:
            acc[...] = product
        else:
            acc[...] += product
    for load in qloads:
        load.start()
    k_rows = rope(acc[:, :HS], cos[...], sin[...]).astype(BF)
    v_rows = acc[:, HS:].astype(BF)
    kvs[:, 0:HS] = jnp.dot(pack, k_rows, preferred_element_type=F32).astype(BF)
    kvs[:, HS:2 * HS] = jnp.dot(pack, v_rows, preferred_element_type=F32).astype(BF)

    pl.semaphore_wait(barrier, 7 + 31)

    sends = []
    for dz in range(1, 4):
        pz = (z + dz) % 4
        sends.append(pltpu.make_async_remote_copy(
            src_ref=kvs.at[pl.ds(pz * 96, 96), :], dst_ref=zin.at[pl.ds(z * 96, 96), :],
            send_sem=zs_sem.at[dz - 1], recv_sem=zr_sem.at[0],
            device_id=device(x, y, pz, c), device_id_type=MESH))
        sends[-1].start()
    pltpu.make_async_copy(
        kvs.at[pl.ds(z * 96, 96), :], zin.at[pl.ds(z * 96, 96), :], zr_sem.at[0]).start()

    def query_block(n):
        qloads[n].wait()
        acc[...] = jnp.zeros_like(acc)

        @pl.loop(0, 4)
        def _(i):
            part = pl.ds(pl.multiple_of(i * (D // 4), D // 4), D // 4)
            acc[...] += jnp.dot(tok_v[:, part], wq_v[n, part, :], preferred_element_type=F32)

        for h in range(2):
            rows = rope(acc[:, h * HS:(h + 1) * HS], cos[...], sin[...]).astype(BF)
            at = 128 + (n * 2 + h) * HS
            qs[:, at:at + HS] = jnp.dot(pack, rows, preferred_element_type=F32).astype(BF)

    def query_send(half):
        cols = pl.ds(0, 640) if half == 0 else pl.ds(640, 512)
        for i, (pz, pc) in enumerate(peers):
            sends.append(pltpu.make_async_remote_copy(
                src_ref=qs.at[pl.ds((pz * 2 + pc) * PACK, PACK), cols],
                dst_ref=qin.at[pl.ds(line * PACK, PACK), cols],
                send_sem=qs_sem.at[half, i], recv_sem=qr_sem.at[half],
                device_id=device(x, y, pz, pc), device_id_type=MESH))
            sends[-1].start()
        pltpu.make_async_copy(
            qs.at[pl.ds(line * PACK, PACK), cols], qin.at[pl.ds(line * PACK, PACK), cols],
            qr_sem.at[half]).start()

    pltpu.make_async_copy(zin, zin, zr_sem.at[0]).wait()
    aout[...] = jnp.dot(perm[...], zin[...], preferred_element_type=F32).astype(BF)
    for i, (px, py, pc) in enumerate(flat):
        sends.append(pltpu.make_async_remote_copy(
            src_ref=aout.at[pl.ds(block_id(px, py, pc) * 16, 16), :],
            dst_ref=ain.at[pl.ds(mine * 16, 16), :],
            send_sem=as_sem.at[i], recv_sem=ar_sem.at[0],
            device_id=device(px, py, z, pc), device_id_type=MESH))
        sends[-1].start()
    pltpu.make_async_copy(
        aout.at[pl.ds(mine * 16, 16), :], ain.at[pl.ds(mine * 16, 16), :], ar_sem.at[0]).start()

    query_block(0)

    pltpu.make_async_copy(ain, ain, ar_sem.at[0]).wait()
    got = ain[:, 2 * HS:].astype(F32)
    want = (lax.broadcasted_iota(jnp.int32, (512, HS), 1) + 1).astype(F32)
    one = jnp.concatenate([
        (got == want).astype(F32), (got == want + 128.0).astype(F32)], axis=1).astype(BF)
    kblk[...] = dot_t(one, ain[:, 0:HS]).astype(BF)
    vblk[...] = dot_t(ain[:, HS:2 * HS], one).astype(BF)

    def at_offset(a, b):
        return (x + a * (1 - c) + b * c) % 4, (y + a * c + b * (1 - c)) % 4

    def piece(q, a, b):
        px, py = at_offset(a, b)
        return (kall if q == 0 else vtall).at[block_id(px, py, c)]

    def source_of(q, a, b):
        if (a, b) == (0, 0):
            return kblk if q == 0 else vblk
        return piece(q, a, b)

    count = [0]

    def push(q, a, b, da, db):
        px, py = at_offset(da, db)
        sends.append(pltpu.make_async_remote_copy(
            src_ref=source_of(q, a, b), dst_ref=piece(q, a, b),
            send_sem=ts_sem.at[count[0]], recv_sem=tr_sem.at[q * 16 + (a - da) % 4 * 4 + (b - db) % 4],
            device_id=device(px, py, z, c), device_id_type=MESH))
        sends[-1].start()
        count[0] += 1

    def share(q, a, b):
        sends.append(pltpu.make_async_remote_copy(
            src_ref=source_of(q, a, b), dst_ref=piece(q, a, b),
            send_sem=ds_sem.at[q * 16 + a * 4 + b], recv_sem=dr_sem.at[q],
            device_id=device(x, y, z, 1 - c), device_id_type=MESH))
        sends[-1].start()

    local = [
        pltpu.make_async_copy(source_of(q, 0, 0), piece(q, 0, 0), loc_sem.at[q]) for q in range(2)]
    for da in (1, 3, 2):
        for q in range(2):
            push(q, 0, 0, da, 0)
    for db in (1, 3):
        for q in range(2):
            push(q, 0, 0, 0, db)
    for q in range(2):
        local[q].start()
        share(q, 0, 0)

    def arrive(q, a, b):
        ref = piece(q, a, b)
        pltpu.make_async_copy(ref, ref, tr_sem.at[q * 16 + a * 4 + b]).wait()
        if b == 0:
            push(q, a, b, 0, 1)
            push(q, a, b, 0, 3)
        elif b == (3, 1)[q]:
            push(q, a, b, 0, (1, 3)[q])
        share(q, a, b)

    query_block(1)
    query_send(0)
    for a, b in ((1, 0), (3, 0), (2, 0)):
        for q in range(2):
            arrive(q, a, b)
    query_block(2)
    for a, b in ((0, 1), (0, 3)):
        for q in range(2):
            arrive(q, a, b)
    query_block(3)
    query_send(1)
    for a, b in ((1, 1), (1, 3), (3, 1), (3, 3)):
        for q in range(2):
            arrive(q, a, b)

    pltpu.make_async_copy(qin.at[:, pl.ds(0, 640)], qin.at[:, pl.ds(0, 640)], qr_sem.at[0]).wait()
    shape = (NPACK, HS)
    i = lax.broadcasted_iota(jnp.int32, shape, 0)
    w = i - ((i * 43691) >> 21) * PACK
    base = ((w * 43691) >> 17) * 2 + c
    m = qin[:, 0:HS].astype(F32)
    slot = jnp.where(m > 0.0, base.astype(F32) * 256.0 + m - 1.0, 8192.0 + i.astype(F32))
    slot_row = jnp.transpose(slot)[0:1, :]
    slot_wide = jnp.concatenate([slot] * 3, axis=1)
    rank = jnp.sum((slot_row < slot_wide).astype(F32), axis=1, keepdims=True)
    lane = lax.broadcasted_iota(jnp.int32, (NPACK, NPACK), 1).astype(F32)
    one_o[...] = (lane == rank).astype(F32).astype(BF)

    for a, b in ((2, 1), (2, 3)):
        for q in range(2):
            arrive(q, a, b)

    rank_wide = jnp.broadcast_to(rank, shape)
    lane_q = (lax.broadcasted_iota(jnp.int32, shape, 1) & (CHUNK - 1)).astype(F32)
    lanes_o[...] = jnp.full_like(lanes_o, 8192)
    for n in range(NCHUNK):
        pick = rank_wide == lane_q + float(n * CHUNK)
        lanes_o[n:n + 1, :] = jnp.sum(
            jnp.where(pick, slot, 0.0), axis=0, keepdims=True).astype(jnp.int32)
    slots = lanes_o[...]
    start = starts(slots, ends)
    for n, v in enumerate((
        jnp.min(start, axis=1, keepdims=True),
        jnp.max(jnp.where(slots < 8192, slots, -1), axis=1, keepdims=True),
        jnp.max(start, axis=1, keepdims=True),
        jnp.min(slots, axis=1, keepdims=True),
    )):
        bounds_o[n * 16:(n + 1) * 16, :] = jnp.broadcast_to(v, (16, HS))
    pltpu.make_async_copy(qin.at[:, pl.ds(640, 512)], qin.at[:, pl.ds(640, 512)], qr_sem.at[1]).wait()
    qsort[...] = dot_t(one_o[...], qin[:, HS:]).astype(BF)

    for a, b in ((0, 2), (1, 2), (3, 2), (2, 2)):
        for q in range(2):
            arrive(q, a, b)
    other = pl.ds((1 - c) * 16, 16)
    pltpu.make_async_copy(kall.at[other], kall.at[other], dr_sem.at[0]).wait()
    pltpu.make_async_copy(vtall.at[other], vtall.at[other], dr_sem.at[1]).wait()
    for copy in local:
        copy.wait()
    for copy in sends:
        copy.wait_send()


def front(ends, tokens, wq, wk, wv, cos, sin, meta, pidx):
    anyspace = pl.BlockSpec(memory_space=pl.ANY)
    vmem = pl.BlockSpec(memory_space=pltpu.VMEM)
    dma = pltpu.SemaphoreType.DMA
    return pl.pallas_call(
        front_kernel,
        out_shape=(
            jax.ShapeDtypeStruct((NBLOCKS, ROWS, HS), BF),
            jax.ShapeDtypeStruct((NBLOCKS, HS, ROWS), BF),
            jax.ShapeDtypeStruct((NPACK, HQ * HS), BF),
            jax.ShapeDtypeStruct((NPACK, NPACK), BF),
            jax.ShapeDtypeStruct((16, HS), jnp.int32),
            jax.ShapeDtypeStruct((64, HS), jnp.int32),
        ),
        in_specs=[pl.BlockSpec(memory_space=pltpu.SMEM)] + [anyspace] * 4 + [vmem] * 4,
        out_specs=(anyspace, anyspace, vmem, vmem, vmem, vmem),
        scratch_shapes=[
            pltpu.VMEM((ROWS, D), BF),
            pltpu.VMEM((D, 2 * HS), BF),
            pltpu.VMEM((4, D, 256), BF),
            pltpu.VMEM((ROWS, 256), F32),
            pltpu.VMEM((NPACK, 3 * HS), BF),
            pltpu.VMEM((NPACK, 3 * HS), BF),
            pltpu.VMEM((512, NPACK), BF),
            pltpu.VMEM((512, 3 * HS), BF),
            pltpu.VMEM((512, 3 * HS), BF),
            pltpu.VMEM((ROWS, HS), BF),
            pltpu.VMEM((HS, ROWS), BF),
            pltpu.VMEM((NPACK, QW), BF),
            pltpu.VMEM((NPACK, QW), BF),
            dma((3, KPARTS)), dma((4,)), dma((3,)), dma((1,)), dma((31,)), dma((1,)),
            dma((2, 7)), dma((2,)), dma((30,)), dma((32,)), dma((32,)), dma((2,)), dma((2,)),
        ],
        compiler_params=pltpu.CompilerParams(
            collective_id=0, has_side_effects=True, vmem_limit_bytes=50 << 20),
        name="front",
    )(ends, tokens, wq, wk, wv, cos, sin, meta, pidx)


def attend_kernel(
    ends, bounds, lanes, qsort, one, kall, vtall, out, k_v, vt_v, osort, s_a, s_b, acc, load_sem,
):
    loads = []
    for g in range(4):
        part = pl.ds(g * 8, 8)
        loads.append((
            pltpu.make_async_copy(kall.at[part], k_v.at[part], load_sem.at[g]),
            pltpu.make_async_copy(vtall.at[part], vt_v.at[part], load_sem.at[4 + g]),
        ))
        for load in loads[g]:
            load.start()
    osort[...] = jnp.zeros_like(osort)
    scale = math.log2(math.e) / math.sqrt(HS)
    wide = CHUNK * HQ

    def chunk(n, ready):
        low, high, start_max, slot_min = (bounds[16 * v + n, 0] for v in range(4))

        need = high // (8 * ROWS) + 1
        for g in range(4):
            @pl.when((g >= ready) & (g < need))
            def _():
                for load in loads[g]:
                    load.wait()

        @pl.when(high >= 0)
        def _():
            rows = pl.ds(pl.multiple_of(n * CHUNK, CHUNK), CHUNK)
            queries = jnp.concatenate(
                [qsort[rows, h * HS:(h + 1) * HS] for h in range(HQ)], axis=0)
            half = lanes[pl.ds(n, 1), :]
            mine = jnp.concatenate([half, half], axis=1)
            begin = starts(mine, ends)

            def scores(t, ref):
                keys = k_v[t]
                ref[...] = lax.dot_general(
                    keys, queries, (((1,), (1,)), ((), ())), preferred_element_type=F32)

            first = low // KT
            last = high // KT + 1
            full_from = jnp.clip((start_max + KT - 1) // KT, first, last)
            full_to = jnp.clip((slot_min + 1) // KT, full_from, last)
            scores(2 * first, s_a)
            scores(2 * first + 1, s_b)
            acc[...] = jnp.zeros_like(acc)

            def tile(masked, t, state):
                top, total = state
                a = s_a[...]
                b = s_b[...]
                if masked:
                    at = lax.broadcasted_iota(jnp.int32, (ROWS, wide), 0)
                    begin_a, mine_a = begin - t * KT, mine - t * KT
                    begin_b, mine_b = begin_a - ROWS, mine_a - ROWS
                    a = jnp.where((at >= begin_a) & (at <= mine_a), a, -1e30)
                    b = jnp.where((at >= begin_b) & (at <= mine_b), b, -1e30)
                new = jnp.maximum(
                    top, jnp.max(jnp.maximum(a, b), axis=0, keepdims=True))
                shift = new * scale
                pa = jnp.exp2(a * scale - shift)
                pb = jnp.exp2(b * scale - shift)
                factor = jnp.exp2(top * scale - shift)
                total = total * factor + jnp.sum(pa + pb, axis=0, keepdims=True)
                after = jnp.minimum(t + 1, NBLOCKS // 2 - 1)
                scores(2 * after, s_a)
                scores(2 * after + 1, s_b)
                acc[...] = acc[...] * factor + (
                    jnp.dot(vt_v[2 * t], pa.astype(BF), preferred_element_type=F32)
                    + jnp.dot(vt_v[2 * t + 1], pb.astype(BF), preferred_element_type=F32))
                return new, total

            state = (jnp.full((1, wide), -1e30, F32), jnp.zeros((1, wide), F32))
            state = lax.fori_loop(first, full_from, functools.partial(tile, True), state)
            state = lax.fori_loop(full_from, full_to, functools.partial(tile, False), state)
            top, total = lax.fori_loop(full_to, last, functools.partial(tile, True), state)
            o = jnp.transpose(acc[...] / total).astype(BF)
            for h in range(HQ):
                osort[rows, h * HS:(h + 1) * HS] = o[h * CHUNK:(h + 1) * CHUNK, :]

        return jnp.maximum(ready, need)

    ready = lax.fori_loop(0, NCHUNK, chunk, 0)
    for g in range(4):
        @pl.when(g >= ready)
        def _():
            for load in loads[g]:
                load.wait()
    out[...] = jnp.dot(one[...], osort[...], preferred_element_type=F32).astype(BF)


def attend(ends, bounds, lanes, qsort, one, kall, vtall):
    vmem = pl.BlockSpec(memory_space=pltpu.VMEM)
    smem = pl.BlockSpec(memory_space=pltpu.SMEM)
    anyspace = pl.BlockSpec(memory_space=pl.ANY)
    wide = CHUNK * HQ
    return pl.pallas_call(
        attend_kernel,
        out_shape=jax.ShapeDtypeStruct((NPACK, HQ * HS), BF),
        in_specs=[smem, smem, vmem, vmem, vmem, anyspace, anyspace],
        out_specs=vmem,
        scratch_shapes=[
            pltpu.VMEM((NBLOCKS, ROWS, HS), BF),
            pltpu.VMEM((NBLOCKS, HS, ROWS), BF),
            pltpu.VMEM((NPACK, HQ * HS), BF),
            pltpu.VMEM((ROWS, wide), F32),
            pltpu.VMEM((ROWS, wide), F32),
            pltpu.VMEM((HS, wide), F32),
            pltpu.SemaphoreType.DMA((8,)),
        ],
        compiler_params=pltpu.CompilerParams(vmem_limit_bytes=40 << 20),
        name="attend",
    )(ends, bounds, lanes, qsort, one, kall, vtall)


def back_kernel(pidx, packed, out, ret, send_sem, recv_sem):
    x, y, z, c = place()
    line = z * 2 + c
    peers = []
    for dz in range(4):
        for dc in range(2):
            if (dz, dc) != (0, 0):
                peers.append(((z + dz) % 4, (c + dc) % 2))
    barrier = pltpu.get_barrier_semaphore()
    for pz, pc in peers:
        pl.semaphore_signal(barrier, inc=1, device_id=device(x, y, pz, pc), device_id_type=MESH)
    pl.semaphore_wait(barrier, 7)
    sends = []
    for i, (pz, pc) in enumerate(peers):
        sends.append(pltpu.make_async_remote_copy(
            src_ref=packed.at[pl.ds((pz * 2 + pc) * PACK, PACK), :],
            dst_ref=ret.at[pl.ds(line * PACK, PACK), :],
            send_sem=send_sem.at[i], recv_sem=recv_sem.at[0],
            device_id=device(x, y, pz, pc), device_id_type=MESH))
        sends[-1].start()
    pltpu.make_async_copy(
        packed.at[pl.ds(line * PACK, PACK), :], ret.at[pl.ds(line * PACK, PACK), :], recv_sem.at[0]).start()
    row = lax.broadcasted_iota(jnp.int32, (NPACK, ROWS), 0)
    pack = (row == pidx[...]).astype(F32).astype(BF)
    pltpu.make_async_copy(ret, ret, recv_sem.at[0]).wait()
    out[...] = dot_t(pack, ret[...]).astype(BF)
    for copy in sends:
        copy.wait_send()


def back(pidx, packed):
    anyspace = pl.BlockSpec(memory_space=pl.ANY)
    vmem = pl.BlockSpec(memory_space=pltpu.VMEM)
    return pl.pallas_call(
        back_kernel,
        out_shape=jax.ShapeDtypeStruct((ROWS, HQ * HS), BF),
        in_specs=[vmem, anyspace],
        out_specs=vmem,
        scratch_shapes=[pltpu.VMEM((NPACK, HQ * HS), BF), pltpu.SemaphoreType.DMA((7,)), pltpu.SemaphoreType.DMA((1,))],
        compiler_params=pltpu.CompilerParams(collective_id=1, has_side_effects=True),
        name="back",
    )(pidx, packed)


def shards(tokens, query_weight, key_weight, value_weight, doc_lengths, slot_index):
    x, y, z, c = place()
    order = jnp.arange(ROWS, dtype=jnp.int32)
    block = slot_index // ROWS
    same = block[:, None] == block[None, :]
    rank = jnp.sum((same & (order[None, :] < order[:, None])).astype(jnp.int32), axis=1)
    group = block // NBLOCKS
    local_block = block % NBLOCKS
    pidx = group * 96 + (local_block % 2) * PACK + (local_block // 2) * CAP + rank
    local = slot_index % (NBLOCKS * ROWS)
    ends = jnp.sum(jnp.where(
        jnp.arange(4)[None, :, None] >= jnp.arange(4)[None, None, :], doc_lengths[:, None, :], 0), axis=2)
    in_group = group[:, None] == jnp.arange(4, dtype=jnp.int32)[None, :]
    start = jnp.zeros_like(local)
    for d in range(3):
        end = jnp.sum(jnp.where(in_group, ends[:, d][None, :], 0), axis=1)
        start = jnp.where(local >= end, end, start)
    position = local - start
    frequency = 500000.0 ** (-(jnp.arange(HS // 2, dtype=F32) * 2.0 / HS))
    angles = position.astype(F32)[:, None] * frequency[None, :]
    cosine = jnp.cos(angles)
    sine = jnp.sin(angles)
    cos = jnp.concatenate([cosine, cosine], axis=1)
    sin = jnp.concatenate([-sine, sine], axis=1)
    meta = jnp.broadcast_to((slot_index % ROWS + 1).astype(BF)[:, None], (ROWS, HS))
    mine = jnp.sum(jnp.where(jnp.arange(4)[:, None] == z, ends, 0), axis=0)
    kall, vtall, qsort, one, lanes, bounds = front(
        mine, tokens, query_weight, key_weight, value_weight, cos, sin, meta, pidx[None, :])
    packed = attend(mine, bounds, lanes, qsort, one, kall, vtall)
    return back(pidx[None, :], packed)


def solution(mesh):
    in_specs = (P(("seq", "blk"), None), P(), P(), P(), P(), P(("seq", "blk")))
    out_specs = P(("seq", "blk"), None)
    return jax.shard_map(shards, mesh=mesh, in_specs=in_specs, out_specs=out_specs, check_vma=False)
```

time: 100 us -> 91.3 us (0.913)
  Pallas kernels: 91.2 us -> 83 us
  matrix products: 2.42 us -> 0 us
  local copies, waits for them, and re-layouts: 2.73 us -> 4.61 us
    pallas_call x1, Pallas kernels: 24.5 us -> 16.6 us  [attend(): pl.pallas_call(attend_kernel, out_shape=jax.ShapeDtypeStruct((NPACK, HQ *...]
    dot_general x1 -> x0, matrix products: 2.42 us -> none  [shards(): return jnp.dot(pick, returned, preferred_element_type=F32).astype(BF)]
    unnamed x4 -> x7, local copies, waits for them, and re-layouts: 2.45 us -> 4.33 us
where the time goes in v2:
time: 91.3 us; the launch traced here: 91 us
  Pallas kernels  83 us (91%)
  local copies, waits for them, and re-layouts  4.61 us (5%)
  other arithmetic  3.29 us (4%)
    pallas_call x1, Pallas kernels, front(): pl.pallas_call(front_kernel, out_shape=(jax.ShapeDtypeStruct((NBLOCKS, RO...  46.5 us
    pallas_call x1, Pallas kernels, back(): pl.pallas_call(back_kernel, out_shape=jax.ShapeDtypeStruct((ROWS, HQ * HS...  19.9 us
    pallas_call x1, Pallas kernels, attend(): pl.pallas_call(attend_kernel, out_shape=jax.ShapeDtypeStruct((NPACK, HQ *...  16.6 us
    unnamed x7, local copies, waits for them, and re-layouts  4.33 us

profile of v2, /device:TPU:1, one launch (start us, length us, event | category | flops | bytes accessed | tf_op | source)
XLA Modules:
  0.0 91.0 jit_solution(7372080077218971733)
XLA Ops:
  0.0 0.8 select_reduce_fusion
  0.9 0.1 select_reduce_fusion.4.ends
  0.9 0.2 slice_reduce_fusion
  1.1 0.7 fusion.9
  1.8 0.2 convert_reduce_fusion
  2.0 0.0 copy-start.2
  2.1 0.1 select_reduce_fusion.1
  2.1 0.7 fusion.3
  2.8 0.1 broadcast_in_dim.98.meta
  2.9 0.5 fusion.1
  3.5 0.1 pad_maximum_fusion
  3.6 46.5 %front.1 = (bf16[32,256,128]{2,1,0:T(8,128)(2,1)S(1)}, bf16[32,128,256]{2,1,0:T(8,128)(2,1)}, bf16[384,1024]{1,0:T(8,128)(2,1)S(1)}, bf16[384,384]{1,0:T(8,128)(...) custom-call(s32[4]{0:T(128)S(1)} %select_reduce_fusion.4.ends, bf16[256,8192]{1,0:T(8,128)(2,1)} %tok.1, ...), custom_call_target="tpu_custom_call" | custom-call | tf_op jit(solution)/shard_map/front/pallas_call | solution.py:315
  50.1 0.0 copy-done.2
  50.1 0.0 copy-start.1
  50.2 1.6 %copy-done.1 = bf16[32,128,256]{2,1,0:T(8,128)(2,1)S(1)} copy-done((bf16[32,128,256]{2,1,0:T(8,128)(2,1)S(1)}, bf16[32,128,256]{2,1,0:T(8,128)(2,1)}, u32[]{:S(2)}) %copy-start.1) | copy-done | bytes 2097176
  51.7 16.6 %attend.1.packed = bf16[384,1024]{1,0:T(8,128)(2,1)S(1)} custom-call(s32[4]{0:T(128)S(1)} %select_reduce_fusion.4.ends, s32[64,128]{1,0:T(8,128)S(1)} %get-tuple-element.11.bounds, s32[16,128]{1,0:T(8,128)S(1)} %get-tuple-element.12.lanes, bf16[384,1024]{1,0:T(8,128)(2,1)S(1)} %get-tuple-element.13.qsort, bf16[384,384]{1,0:T(8,128)(2,1)S(1)} %get-tuple-element.14.one, ...), custom_call_target="tpu_custom_call" | custom-call | tf_op jit(solution)/shard_map/attend/pallas_call | solution.py:447
  68.4 0.0 copy-start
  68.4 0.9 copy-done
  69.3 19.9 %back.1 = bf16[256,1024]{1,0:T(8,128)(2,1)} custom-call(s32[1,256]{1,0:T(1,128)} %bitcast.2, bf16[384,1024]{1,0:T(8,128)(2,1)} %copy-done), custom_call_target="tpu_custom_call" | custom-call | tf_op jit(solution)/shard_map/back/pallas_call | solution.py:499
  89.2 1.9 %copy.8 = bf16[256,1024]{1,0:T(8,128)(2,1)} copy(bf16[256,1024]{1,0:T(8,128)(2,1)} %back.1) | data formatting | bytes 1048576
  (4 shorter events, 0.0 us)
Async XLA Ops:
  2.0 48.1 %copy-start.2 = (s32[256]{0:T(256)}, s32[256]{0:T(256)S(1)}, u32[]{:S(2)}) copy-start(s32[256]{0:T(256)S(1)} %get-tuple-element.23) | copy-start | bytes 3076
  50.1 1.6 %copy-start.1 = (bf16[32,128,256]{2,1,0:T(8,128)(2,1)S(1)}, bf16[32,128,256]{2,1,0:T(8,128)(2,1)}, u32[]{:S(2)}) copy-start(bf16[32,128,256]{2,1,0:T(8,128)(2,1)} %get-tuple-element.16.vtall) | copy-start | bytes 6291460
  68.4 0.9 copy-start

commit v3 on v2

--- a/solution.py
+++ b/solution.py
@@ -51,17 +51,10 @@
     return v * cos + pltpu.roll(v, HS // 2, 1) * sin
 
 
-def starts(slots, ends):
-    start = jnp.zeros_like(slots)
-    for d in range(3):
-        start = jnp.where(slots >= ends[d], ends[d], start)
-    return start
-
-
 def front_kernel(
-    ends, tok, wq, wk, wv, cos, sin, meta, pidx,
-    kall, vtall, qsort, one_o, lanes_o, bounds_o,
-    tok_v, wkv_v, wq_v, acc, kvs, zin, perm, aout, ain, kblk, vblk, qs, qin,
+    lengths, slot_ref, freq, tok, wq, wk, wv,
+    kall, vtall, qsort, one_o, lanes_o, bounds_o, pack_o,
+    cos, sin, tok_v, wkv_v, wq_v, acc, kvs, zin, perm, aout, ain, kblk, vblk, qs, qin,
     tok_sem, wq_sem, zs_sem, zr_sem, as_sem, ar_sem, qs_sem, qr_sem,
     ts_sem, tr_sem, ds_sem, dr_sem, loc_sem,
 ):
@@ -102,18 +95,34 @@
     for px, py, pc in flat:
         pl.semaphore_signal(barrier, inc=1, device_id=device(px, py, z, pc), device_id_type=MESH)
 
+    slot_r = slot_ref[...]
+    block_r = slot_r >> 8
+    slot_c = jnp.transpose(jnp.broadcast_to(slot_r.astype(F32), (HS, ROWS))).astype(jnp.int32)
+    block_c = slot_c >> 8
+    block_w = jnp.concatenate([block_c, block_c], axis=1)
+    earlier = lax.broadcasted_iota(jnp.int32, (ROWS, ROWS), 0) < lax.broadcasted_iota(jnp.int32, (ROWS, ROWS), 1)
+    rank_r = jnp.sum(
+        ((block_w == block_r) & earlier).astype(F32), axis=0, keepdims=True).astype(jnp.int32)
+    pidx = (block_r >> 5) * 96 + (block_r & 1) * PACK + ((block_r & 31) >> 1) * CAP + rank_r
     lane = lax.broadcasted_iota(jnp.int32, (NPACK, ROWS), 0)
-    pack = (lane == pidx[...]).astype(F32).astype(BF)
-    row = lax.broadcasted_iota(jnp.int32, (512, NPACK), 0)
-    col = lax.broadcasted_iota(jnp.int32, (512, NPACK), 1)
-    j = row >> 4
-    slot12 = row & 15
-    zz = (slot12 >= 3).astype(jnp.int32) + (slot12 >= 6).astype(jnp.int32) + (slot12 >= 9).astype(jnp.int32)
-    source = zz * 96 + (j & 1) * 48 + (j >> 1) * 3 + (slot12 - 3 * zz)
-    perm[...] = ((source == col) & (slot12 < 12)).astype(F32).astype(BF)
-    slots = jnp.dot(pack, meta[...], preferred_element_type=F32).astype(BF)
+    pack = (lane == pidx).astype(F32).astype(BF)
+    pack_o[...] = pack
+    meta = ((slot_c & 255) + 1).astype(F32).astype(BF)
+    slots = jnp.dot(pack, meta, preferred_element_type=F32).astype(BF)
     kvs[:, 2 * HS:] = slots
     qs[:, 0:128] = slots
+    local_c = slot_c & 8191
+    group_c = slot_c >> 13
+    start_c = jnp.zeros_like(slot_c)
+    for g in range(4):
+        end = 0
+        for d in range(3):
+            end = end + lengths[g, d]
+            start_c = jnp.where((group_c == g) & (local_c >= end), end, start_c)
+    angle = (local_c - start_c).astype(F32) * freq[...]
+    cos[...] = jnp.cos(angle)
+    sine = jnp.sin(angle)
+    sin[...] = jnp.where(lax.broadcasted_iota(jnp.int32, (ROWS, HS), 1) < HS // 2, -sine, sine)
 
     for i in range(KPARTS):
         part = pl.ds(i * kc, kc)
@@ -144,6 +153,37 @@
     pltpu.make_async_copy(
         kvs.at[pl.ds(z * 96, 96), :], zin.at[pl.ds(z * 96, 96), :], zr_sem.at[0]).start()
 
+    def query_send(part):
+        cols = (pl.ds(0, 128), pl.ds(128, 512), pl.ds(640, 512))[part]
+        for i, (pz, pc) in enumerate(peers):
+            sends.append(pltpu.make_async_remote_copy(
+                src_ref=qs.at[pl.ds((pz * 2 + pc) * PACK, PACK), cols],
+                dst_ref=qin.at[pl.ds(line * PACK, PACK), cols],
+                send_sem=qs_sem.at[part, i], recv_sem=qr_sem.at[part],
+                device_id=device(x, y, pz, pc), device_id_type=MESH))
+            sends[-1].start()
+        pltpu.make_async_copy(
+            qs.at[pl.ds(line * PACK, PACK), cols], qin.at[pl.ds(line * PACK, PACK), cols],
+            qr_sem.at[part]).start()
+
+    def query_wait(part):
+        cols = (pl.ds(0, 128), pl.ds(128, 512), pl.ds(640, 512))[part]
+        pltpu.make_async_copy(qin.at[:, cols], qin.at[:, cols], qr_sem.at[part]).wait()
+
+    def flush():
+        while sends:
+            sends.pop(0).wait_send()
+
+    query_send(0)
+
+    row = lax.broadcasted_iota(jnp.int32, (512, NPACK), 0)
+    col = lax.broadcasted_iota(jnp.int32, (512, NPACK), 1)
+    j = row >> 4
+    slot12 = row & 15
+    zz = (slot12 >= 3).astype(jnp.int32) + (slot12 >= 6).astype(jnp.int32) + (slot12 >= 9).astype(jnp.int32)
+    source = zz * 96 + (j & 1) * 48 + (j >> 1) * 3 + (slot12 - 3 * zz)
+    perm[...] = ((source == col) & (slot12 < 12)).astype(F32).astype(BF)
+
     def query_block(n):
         qloads[n].wait()
         acc[...] = jnp.zeros_like(acc)
@@ -158,18 +198,7 @@
             at = 128 + (n * 2 + h) * HS
             qs[:, at:at + HS] = jnp.dot(pack, rows, preferred_element_type=F32).astype(BF)
 
-    def query_send(half):
-        cols = pl.ds(0, 640) if half == 0 else pl.ds(640, 512)
-        for i, (pz, pc) in enumerate(peers):
-            sends.append(pltpu.make_async_remote_copy(
-                src_ref=qs.at[pl.ds((pz * 2 + pc) * PACK, PACK), cols],
-                dst_ref=qin.at[pl.ds(line * PACK, PACK), cols],
-                send_sem=qs_sem.at[half, i], recv_sem=qr_sem.at[half],
-                device_id=device(x, y, pz, pc), device_id_type=MESH))
-            sends[-1].start()
-        pltpu.make_async_copy(
-            qs.at[pl.ds(line * PACK, PACK), cols], qin.at[pl.ds(line * PACK, PACK), cols],
-            qr_sem.at[half]).start()
+    query_block(0)
 
     pltpu.make_async_copy(zin, zin, zr_sem.at[0]).wait()
     aout[...] = jnp.dot(perm[...], zin[...], preferred_element_type=F32).astype(BF)
@@ -183,7 +212,46 @@
     pltpu.make_async_copy(
         aout.at[pl.ds(mine * 16, 16), :], ain.at[pl.ds(mine * 16, 16), :], ar_sem.at[0]).start()
 
-    query_block(0)
+    query_block(1)
+    query_send(1)
+    query_block(2)
+
+    query_wait(0)
+    shape = (NPACK, HS)
+    i = lax.broadcasted_iota(jnp.int32, shape, 0)
+    w = i - ((i * 43691) >> 21) * PACK
+    base = ((w * 43691) >> 17) * 2 + c
+    m = qin[:, 0:HS].astype(F32)
+    slot = jnp.where(m > 0.0, base.astype(F32) * 256.0 + m - 1.0, 8192.0 + i.astype(F32))
+    slot_row = jnp.transpose(slot)[0:1, :]
+    slot_wide = jnp.concatenate([slot] * 3, axis=1)
+    rank = jnp.sum((slot_row < slot_wide).astype(F32), axis=1, keepdims=True)
+    lane = lax.broadcasted_iota(jnp.int32, (NPACK, NPACK), 1).astype(F32)
+    one_o[...] = (lane == rank).astype(F32).astype(BF)
+    rank_wide = jnp.broadcast_to(rank, shape)
+    lane_q = (lax.broadcasted_iota(jnp.int32, shape, 1) & (CHUNK - 1)).astype(F32)
+    lanes_o[0:16, :] = jnp.full((16, HS), 8192, jnp.int32)
+    for n in range(NCHUNK):
+        pick = rank_wide == lane_q + float(n * CHUNK)
+        lanes_o[n:n + 1, :] = jnp.sum(
+            jnp.where(pick, slot, 0.0), axis=0, keepdims=True).astype(jnp.int32)
+    slots = lanes_o[0:16, :]
+    start = jnp.zeros_like(slots)
+    end = 0
+    for d in range(3):
+        end = end + lengths[z, d]
+        start = jnp.where(slots >= end, end, start)
+    lanes_o[16:32, :] = start
+    for n, v in enumerate((
+        jnp.min(start, axis=1, keepdims=True),
+        jnp.max(jnp.where(slots < 8192, slots, -1), axis=1, keepdims=True),
+        jnp.max(start, axis=1, keepdims=True),
+        jnp.min(slots, axis=1, keepdims=True),
+    )):
+        bounds_o[n * 16:(n + 1) * 16, :] = jnp.broadcast_to(v, (16, HS))
+
+    query_block(3)
+    query_send(2)
 
     pltpu.make_async_copy(ain, ain, ar_sem.at[0]).wait()
     got = ain[:, 2 * HS:].astype(F32)
@@ -245,57 +313,14 @@
             push(q, a, b, 0, (1, 3)[q])
         share(q, a, b)
 
-    query_block(1)
-    query_send(0)
-    for a, b in ((1, 0), (3, 0), (2, 0)):
+    for a, b in ((1, 0), (3, 0), (0, 1), (0, 3), (2, 0), (1, 1), (1, 3), (3, 1), (3, 3), (2, 1), (2, 3)):
         for q in range(2):
             arrive(q, a, b)
-    query_block(2)
-    for a, b in ((0, 1), (0, 3)):
-        for q in range(2):
-            arrive(q, a, b)
-    query_block(3)
-    query_send(1)
-    for a, b in ((1, 1), (1, 3), (3, 1), (3, 3)):
-        for q in range(2):
-            arrive(q, a, b)
-
-    pltpu.make_async_copy(qin.at[:, pl.ds(0, 640)], qin.at[:, pl.ds(0, 640)], qr_sem.at[0]).wait()
-    shape = (NPACK, HS)
-    i = lax.broadcasted_iota(jnp.int32, shape, 0)
-    w = i - ((i * 43691) >> 21) * PACK
-    base = ((w * 43691) >> 17) * 2 + c
-    m = qin[:, 0:HS].astype(F32)
-    slot = jnp.where(m > 0.0, base.astype(F32) * 256.0 + m - 1.0, 8192.0 + i.astype(F32))
-    slot_row = jnp.transpose(slot)[0:1, :]
-    slot_wide = jnp.concatenate([slot] * 3, axis=1)
-    rank = jnp.sum((slot_row < slot_wide).astype(F32), axis=1, keepdims=True)
-    lane = lax.broadcasted_iota(jnp.int32, (NPACK, NPACK), 1).astype(F32)
-    one_o[...] = (lane == rank).astype(F32).astype(BF)
-
-    for a, b in ((2, 1), (2, 3)):
-        for q in range(2):
-            arrive(q, a, b)
-
-    rank_wide = jnp.broadcast_to(rank, shape)
-    lane_q = (lax.broadcasted_iota(jnp.int32, shape, 1) & (CHUNK - 1)).astype(F32)
-    lanes_o[...] = jnp.full_like(lanes_o, 8192)
-    for n in range(NCHUNK):
-        pick = rank_wide == lane_q + float(n * CHUNK)
-        lanes_o[n:n + 1, :] = jnp.sum(
-            jnp.where(pick, slot, 0.0), axis=0, keepdims=True).astype(jnp.int32)
-    slots = lanes_o[...]
-    start = starts(slots, ends)
-    for n, v in enumerate((
-        jnp.min(start, axis=1, keepdims=True),
-        jnp.max(jnp.where(slots < 8192, slots, -1), axis=1, keepdims=True),
-        jnp.max(start, axis=1, keepdims=True),
-        jnp.min(slots, axis=1, keepdims=True),
-    )):
-        bounds_o[n * 16:(n + 1) * 16, :] = jnp.broadcast_to(v, (16, HS))
-    pltpu.make_async_copy(qin.at[:, pl.ds(640, 512)], qin.at[:, pl.ds(640, 512)], qr_sem.at[1]).wait()
+    query_wait(1)
+    query_wait(2)
     qsort[...] = dot_t(one_o[...], qin[:, HS:]).astype(BF)
-
+    while len(sends) > 36:
+        sends.pop(0).wait_send()
     for a, b in ((0, 2), (1, 2), (3, 2), (2, 2)):
         for q in range(2):
             arrive(q, a, b)
@@ -304,11 +329,10 @@
     pltpu.make_async_copy(vtall.at[other], vtall.at[other], dr_sem.at[1]).wait()
     for copy in local:
         copy.wait()
-    for copy in sends:
-        copy.wait_send()
-
-
-def front(ends, tokens, wq, wk, wv, cos, sin, meta, pidx):
+    flush()
+
+
+def front(lengths, slot_row, freq, tokens, wq, wk, wv):
     anyspace = pl.BlockSpec(memory_space=pl.ANY)
     vmem = pl.BlockSpec(memory_space=pltpu.VMEM)
     dma = pltpu.SemaphoreType.DMA
@@ -319,12 +343,15 @@
             jax.ShapeDtypeStruct((NBLOCKS, HS, ROWS), BF),
             jax.ShapeDtypeStruct((NPACK, HQ * HS), BF),
             jax.ShapeDtypeStruct((NPACK, NPACK), BF),
-            jax.ShapeDtypeStruct((16, HS), jnp.int32),
+            jax.ShapeDtypeStruct((32, HS), jnp.int32),
             jax.ShapeDtypeStruct((64, HS), jnp.int32),
+            jax.ShapeDtypeStruct((NPACK, ROWS), BF),
         ),
-        in_specs=[pl.BlockSpec(memory_space=pltpu.SMEM)] + [anyspace] * 4 + [vmem] * 4,
-        out_specs=(anyspace, anyspace, vmem, vmem, vmem, vmem),
+        in_specs=[pl.BlockSpec(memory_space=pltpu.SMEM), vmem, vmem] + [anyspace] * 4,
+        out_specs=(anyspace, anyspace, vmem, vmem, vmem, vmem, vmem),
         scratch_shapes=[
+            pltpu.VMEM((ROWS, HS), F32),
+            pltpu.VMEM((ROWS, HS), F32),
             pltpu.VMEM((ROWS, D), BF),
             pltpu.VMEM((D, 2 * HS), BF),
             pltpu.VMEM((4, D, 256), BF),
@@ -339,39 +366,23 @@
             pltpu.VMEM((NPACK, QW), BF),
             pltpu.VMEM((NPACK, QW), BF),
             dma((3, KPARTS)), dma((4,)), dma((3,)), dma((1,)), dma((31,)), dma((1,)),
-            dma((2, 7)), dma((2,)), dma((30,)), dma((32,)), dma((32,)), dma((2,)), dma((2,)),
+            dma((3, 7)), dma((3,)), dma((30,)), dma((32,)), dma((32,)), dma((2,)), dma((2,)),
         ],
         compiler_params=pltpu.CompilerParams(
-            collective_id=0, has_side_effects=True, vmem_limit_bytes=50 << 20),
+            collective_id=0, has_side_effects=True, vmem_limit_bytes=47 << 20),
         name="front",
-    )(ends, tokens, wq, wk, wv, cos, sin, meta, pidx)
+    )(lengths, slot_row, freq, tokens, wq, wk, wv)
 
 
 def attend_kernel(
-    ends, bounds, lanes, qsort, one, kall, vtall, out, k_v, vt_v, osort, s_a, s_b, acc, load_sem,
+    bounds, lanes, qsort, one, k_v, vt_v, out, osort, s_a, s_b, acc,
 ):
-    loads = []
-    for g in range(4):
-        part = pl.ds(g * 8, 8)
-        loads.append((
-            pltpu.make_async_copy(kall.at[part], k_v.at[part], load_sem.at[g]),
-            pltpu.make_async_copy(vtall.at[part], vt_v.at[part], load_sem.at[4 + g]),
-        ))
-        for load in loads[g]:
-            load.start()
     osort[...] = jnp.zeros_like(osort)
     scale = math.log2(math.e) / math.sqrt(HS)
     wide = CHUNK * HQ
 
-    def chunk(n, ready):
+    def chunk(n, carry):
         low, high, start_max, slot_min = (bounds[16 * v + n, 0] for v in range(4))
-
-        need = high // (8 * ROWS) + 1
-        for g in range(4):
-            @pl.when((g >= ready) & (g < need))
-            def _():
-                for load in loads[g]:
-                    load.wait()
 
         @pl.when(high >= 0)
         def _():
@@ -380,7 +391,8 @@
                 [qsort[rows, h * HS:(h + 1) * HS] for h in range(HQ)], axis=0)
             half = lanes[pl.ds(n, 1), :]
             mine = jnp.concatenate([half, half], axis=1)
-            begin = starts(mine, ends)
+            half = lanes[pl.ds(n + 16, 1), :]
+            begin = jnp.concatenate([half, half], axis=1)
 
             def scores(t, ref):
                 keys = k_v[t]
@@ -428,42 +440,33 @@
             for h in range(HQ):
                 osort[rows, h * HS:(h + 1) * HS] = o[h * CHUNK:(h + 1) * CHUNK, :]
 
-        return jnp.maximum(ready, need)
-
-    ready = lax.fori_loop(0, NCHUNK, chunk, 0)
-    for g in range(4):
-        @pl.when(g >= ready)
-        def _():
-            for load in loads[g]:
-                load.wait()
+        return carry
+
+    lax.fori_loop(0, NCHUNK, chunk, 0)
     out[...] = jnp.dot(one[...], osort[...], preferred_element_type=F32).astype(BF)
 
 
-def attend(ends, bounds, lanes, qsort, one, kall, vtall):
+def attend(bounds, lanes, qsort, one, kall, vtall):
     vmem = pl.BlockSpec(memory_space=pltpu.VMEM)
     smem = pl.BlockSpec(memory_space=pltpu.SMEM)
-    anyspace = pl.BlockSpec(memory_space=pl.ANY)
     wide = CHUNK * HQ
     return pl.pallas_call(
         attend_kernel,
         out_shape=jax.ShapeDtypeStruct((NPACK, HQ * HS), BF),
-        in_specs=[smem, smem, vmem, vmem, vmem, anyspace, anyspace],
+        in_specs=[smem, vmem, vmem, vmem, vmem, vmem],
         out_specs=vmem,
         scratch_shapes=[
-            pltpu.VMEM((NBLOCKS, ROWS, HS), BF),
-            pltpu.VMEM((NBLOCKS, HS, ROWS), BF),
             pltpu.VMEM((NPACK, HQ * HS), BF),
             pltpu.VMEM((ROWS, wide), F32),
             pltpu.VMEM((ROWS, wide), F32),
             pltpu.VMEM((HS, wide), F32),
-            pltpu.SemaphoreType.DMA((8,)),
         ],
-        compiler_params=pltpu.CompilerParams(vmem_limit_bytes=40 << 20),
+        compiler_params=pltpu.CompilerParams(vmem_limit_bytes=16 << 20),
         name="attend",
-    )(ends, bounds, lanes, qsort, one, kall, vtall)
-
-
-def back_kernel(pidx, packed, out, ret, send_sem, recv_sem):
+    )(bounds, lanes, qsort, one, kall, vtall)
+
+
+def back_kernel(packed, ret, send_sem, recv_sem):
     x, y, z, c = place()
     line = z * 2 + c
     peers = []
@@ -485,58 +488,47 @@
         sends[-1].start()
     pltpu.make_async_copy(
         packed.at[pl.ds(line * PACK, PACK), :], ret.at[pl.ds(line * PACK, PACK), :], recv_sem.at[0]).start()
-    row = lax.broadcasted_iota(jnp.int32, (NPACK, ROWS), 0)
-    pack = (row == pidx[...]).astype(F32).astype(BF)
     pltpu.make_async_copy(ret, ret, recv_sem.at[0]).wait()
-    out[...] = dot_t(pack, ret[...]).astype(BF)
     for copy in sends:
         copy.wait_send()
 
 
-def back(pidx, packed):
-    anyspace = pl.BlockSpec(memory_space=pl.ANY)
+def back(packed):
     vmem = pl.BlockSpec(memory_space=pltpu.VMEM)
     return pl.pallas_call(
         back_kernel,
+        out_shape=jax.ShapeDtypeStruct((NPACK, HQ * HS), BF),
+        in_specs=[vmem],
+        out_specs=pl.BlockSpec(memory_space=pl.ANY),
+        scratch_shapes=[pltpu.SemaphoreType.DMA((7,)), pltpu.SemaphoreType.DMA((1,))],
+        compiler_params=pltpu.CompilerParams(collective_id=1, has_side_effects=True, vmem_limit_bytes=4 << 20),
+        name="back",
+    )(packed)
+
+
+def finish_kernel(pack, ret, out):
+    out[...] = dot_t(pack[...], ret[...]).astype(BF)
+
+
+def finish(pack, ret):
+    vmem = pl.BlockSpec(memory_space=pltpu.VMEM)
+    return pl.pallas_call(
+        finish_kernel,
         out_shape=jax.ShapeDtypeStruct((ROWS, HQ * HS), BF),
-        in_specs=[vmem, anyspace],
+        in_specs=[vmem, vmem],
         out_specs=vmem,
-        scratch_shapes=[pltpu.VMEM((NPACK, HQ * HS), BF), pltpu.SemaphoreType.DMA((7,)), pltpu.SemaphoreType.DMA((1,))],
-        compiler_params=pltpu.CompilerParams(collective_id=1, has_side_effects=True),
-        name="back",
-    )(pidx, packed)
+        compiler_params=pltpu.CompilerParams(vmem_limit_bytes=8 << 20),
+        name="finish",
+    )(pack, ret)
 
 
 def shards(tokens, query_weight, key_weight, value_weight, doc_lengths, slot_index):
-    x, y, z, c = place()
-    order = jnp.arange(ROWS, dtype=jnp.int32)
-    block = slot_index // ROWS
-    same = block[:, None] == block[None, :]
-    rank = jnp.sum((same & (order[None, :] < order[:, None])).astype(jnp.int32), axis=1)
-    group = block // NBLOCKS
-    local_block = block % NBLOCKS
-    pidx = group * 96 + (local_block % 2) * PACK + (local_block // 2) * CAP + rank
-    local = slot_index % (NBLOCKS * ROWS)
-    ends = jnp.sum(jnp.where(
-        jnp.arange(4)[None, :, None] >= jnp.arange(4)[None, None, :], doc_lengths[:, None, :], 0), axis=2)
-    in_group = group[:, None] == jnp.arange(4, dtype=jnp.int32)[None, :]
-    start = jnp.zeros_like(local)
-    for d in range(3):
-        end = jnp.sum(jnp.where(in_group, ends[:, d][None, :], 0), axis=1)
-        start = jnp.where(local >= end, end, start)
-    position = local - start
     frequency = 500000.0 ** (-(jnp.arange(HS // 2, dtype=F32) * 2.0 / HS))
-    angles = position.astype(F32)[:, None] * frequency[None, :]
-    cosine = jnp.cos(angles)
-    sine = jnp.sin(angles)
-    cos = jnp.concatenate([cosine, cosine], axis=1)
-    sin = jnp.concatenate([-sine, sine], axis=1)
-    meta = jnp.broadcast_to((slot_index % ROWS + 1).astype(BF)[:, None], (ROWS, HS))
-    mine = jnp.sum(jnp.where(jnp.arange(4)[:, None] == z, ends, 0), axis=0)
-    kall, vtall, qsort, one, lanes, bounds = front(
-        mine, tokens, query_weight, key_weight, value_weight, cos, sin, meta, pidx[None, :])
-    packed = attend(mine, bounds, lanes, qsort, one, kall, vtall)
-    return back(pidx[None, :], packed)
+    frequency = jnp.concatenate([frequency, frequency])[None, :]
+    kall, vtall, qsort, one, lanes, bounds, pack = front(
+        doc_lengths, slot_index[None, :], frequency, tokens, query_weight, key_weight, value_weight)
+    packed = attend(bounds, lanes, qsort, one, kall, vtall)
+    return finish(pack, back(packed))
 
 
 def solution(mesh):

time: 91.3 us -> 80.8 us (0.88)
  Pallas kernels: 83 us -> 79.2 us
  local copies, waits for them, and re-layouts: 4.61 us -> 1.36 us
  other arithmetic: 3.29 us -> 0.09 us
    pallas_call x1 -> x2, Pallas kernels: 19.9 us -> 14.9 us  [the longest x1 13.6 us: back(): pl.pallas_call(back_kernel, out_shape=jax.ShapeDtypeStruct((NPACK, HQ * H...]
    pallas_call x1, Pallas kernels: 16.6 us -> 20.8 us  [attend(): pl.pallas_call(attend_kernel, out_shape=jax.ShapeDtypeStruct((NPACK, HQ *...]
    pallas_call x1, Pallas kernels: 46.5 us -> 43.5 us  [front(): pl.pallas_call(front_kernel, out_shape=(jax.ShapeDtypeStruct((NBLOCKS, RO...]
    unnamed x7 -> x4, local copies, waits for them, and re-layouts: 4.33 us -> 1.36 us
    convert_element_type x2 -> x0, other arithmetic: 1.39 us -> none  [the longest x1 0.7 us: shards(): (slot_index % ROWS + 1).astype(BF)[:, None]]
    reduce_sum x4 -> x0, other arithmetic: 1.18 us -> none  [the longest x1 0.82 us: shards(): jnp.sum(jnp.where(jnp.arange(4)[None, :, None] >= jnp.arange(4)[None, Non...]
where the time goes in v3:
time: 80.8 us; the launch traced here: 80.7 us
  Pallas kernels  79.2 us (98%)
  local copies, waits for them, and re-layouts  1.36 us (2%)
    pallas_call x1, Pallas kernels, front(): pl.pallas_call(front_kernel, out_shape=(jax.ShapeDtypeStruct((NBLOCKS, RO...  43.5 us
    pallas_call x1, Pallas kernels, attend(): pl.pallas_call(attend_kernel, out_shape=jax.ShapeDtypeStruct((NPACK, HQ *...  20.8 us
    pallas_call x1, Pallas kernels, back(): pl.pallas_call(back_kernel, out_shape=jax.ShapeDtypeStruct((NPACK, HQ * H...  13.6 us

profile of v3, /device:TPU:1, one launch (start us, length us, event | category | flops | bytes accessed | tf_op | source)
XLA Modules:
  0.0 80.7 jit_solution(6722663415129731852)
XLA Ops:
  0.0 0.1 maximum_bitcast_fusion.freq
  0.1 0.0 copy-start
  0.1 0.7 copy-done
  0.8 0.0 copy-start.1
  0.8 0.7 copy-done.1
  1.5 43.5 %front.1 = (bf16[32,256,128]{2,1,0:T(8,128)(2,1)S(1)}, bf16[32,128,256]{2,1,0:T(8,128)(2,1)S(1)}, bf16[384,1024]{1,0:T(8,128)(2,1)S(1)}, bf16[384,384]{1,0:T(8,1...) custom-call(s32[4,4]{1,0:T(4,128)S(1)} %copy-done, ...), custom_call_target="tpu_custom_call" | custom-call | tf_op jit(solution)/shard_map/front/pallas_call | solution.py:339
  44.9 20.8 %attend.1.packed = bf16[384,1024]{1,0:T(8,128)(2,1)S(1)} custom-call(s32[64,128]{1,0:T(8,128)S(1)} %get-tuple-element.13.bounds, s32[32,128]{1,0:T(8,128)S(1)} %get-tuple-element.14.lanes, bf16[384,1024]{1,0:T(8,128)(2,1)S(1)} %get-tuple-element.15.qsort, bf16[384,384]{1,0:T(8,128)(2,1)S(1)} %get-tuple-element.16.one, ...), custom_call_target="tpu_custom_call" | custom-call | tf_op jit(solution)/shard_map/attend/pallas_call | solution.py:453
  65.8 13.6 %back.1.ret = bf16[384,1024]{1,0:T(8,128)(2,1)S(1)} custom-call(bf16[384,1024]{1,0:T(8,128)(2,1)S(1)} %attend.1.packed), custom_call_target="tpu_custom_call" | custom-call | tf_op jit(solution)/shard_map/back/pallas_call | solution.py:498
  79.4 1.3 %finish.1 = bf16[256,1024]{1,0:T(8,128)(2,1)} custom-call(bf16[384,256]{1,0:T(8,128)(2,1)S(1)} %get-tuple-element.12.pack, bf16[384,1024]{1,0:T(8,128)(2,1)S(1)} %back.1.ret), custom_call_target="tpu_custom_call" | custom-call | tf_op jit(solution)/shard_map/finish/pallas_call | solution.py:515
  (1 shorter events, 0.0 us)
Async XLA Ops:
  0.1 0.7 copy-start
  0.8 0.7 copy-start.1

commit v4 on v3

--- a/solution.py
+++ b/solution.py
@@ -17,7 +17,7 @@
 PACK = 48
 NPACK = 8 * PACK
 QW = 128 + HQ * HS
-KT = 512
+KT = 1024
 KPARTS = 8
 CHUNK = 32
 NCHUNK = NPACK // CHUNK
@@ -52,17 +52,23 @@
 
 
 def front_kernel(
-    lengths, slot_ref, freq, tok, wq, wk, wv,
+    lengths_ref, slot_hbm, freq, tok, wq, wk, wv,
     kall, vtall, qsort, one_o, lanes_o, bounds_o, pack_o,
-    cos, sin, tok_v, wkv_v, wq_v, acc, kvs, zin, perm, aout, ain, kblk, vblk, qs, qin,
+    lengths, slot_ref, cos, sin, tok_v, wkv_v, wq_v, acc, kvs, zin, perm, aout, ain, kblk, vblk, qs, qin,
     tok_sem, wq_sem, zs_sem, zr_sem, as_sem, ar_sem, qs_sem, qr_sem,
-    ts_sem, tr_sem, ds_sem, dr_sem, loc_sem,
+    ts_sem, tr_sem, ds_sem, dr_sem, loc_sem, small_sem,
 ):
     x, y, z, c = place()
     kc = D // KPARTS
     mine = block_id(x, y, c)
     line = z * 2 + c
 
+    small = [
+        pltpu.make_async_copy(lengths_ref, lengths, small_sem.at[0]),
+        pltpu.make_async_copy(slot_hbm, slot_ref, small_sem.at[1]),
+    ]
+    for load in small:
+        load.start()
     loads = []
     for i in range(KPARTS):
         part = pl.ds(i * kc, kc)
@@ -95,6 +101,8 @@
     for px, py, pc in flat:
         pl.semaphore_signal(barrier, inc=1, device_id=device(px, py, z, pc), device_id_type=MESH)
 
+    for load in small:
+        load.wait()
     slot_r = slot_ref[...]
     block_r = slot_r >> 8
     slot_c = jnp.transpose(jnp.broadcast_to(slot_r.astype(F32), (HS, ROWS))).astype(jnp.int32)
@@ -222,7 +230,7 @@
     w = i - ((i * 43691) >> 21) * PACK
     base = ((w * 43691) >> 17) * 2 + c
     m = qin[:, 0:HS].astype(F32)
-    slot = jnp.where(m > 0.0, base.astype(F32) * 256.0 + m - 1.0, 8192.0 + i.astype(F32))
+    slot = jnp.where(m > 0.0, base.astype(F32) * 256.0 + m - 1.0, -1.0 - i.astype(F32))
     slot_row = jnp.transpose(slot)[0:1, :]
     slot_wide = jnp.concatenate([slot] * 3, axis=1)
     rank = jnp.sum((slot_row < slot_wide).astype(F32), axis=1, keepdims=True)
@@ -230,7 +238,7 @@
     one_o[...] = (lane == rank).astype(F32).astype(BF)
     rank_wide = jnp.broadcast_to(rank, shape)
     lane_q = (lax.broadcasted_iota(jnp.int32, shape, 1) & (CHUNK - 1)).astype(F32)
-    lanes_o[0:16, :] = jnp.full((16, HS), 8192, jnp.int32)
+    lanes_o[0:16, :] = jnp.full((16, HS), -1, jnp.int32)
     for n in range(NCHUNK):
         pick = rank_wide == lane_q + float(n * CHUNK)
         lanes_o[n:n + 1, :] = jnp.sum(
@@ -243,10 +251,10 @@
         start = jnp.where(slots >= end, end, start)
     lanes_o[16:32, :] = start
     for n, v in enumerate((
-        jnp.min(start, axis=1, keepdims=True),
-        jnp.max(jnp.where(slots < 8192, slots, -1), axis=1, keepdims=True),
-        jnp.max(start, axis=1, keepdims=True),
-        jnp.min(slots, axis=1, keepdims=True),
+        jnp.min(jnp.where(slots >= 0, start, 8192), axis=1, keepdims=True),
+        jnp.max(slots, axis=1, keepdims=True),
+        jnp.max(jnp.where(slots >= 0, start, 0), axis=1, keepdims=True),
+        jnp.min(jnp.where(slots >= 0, slots, 8192), axis=1, keepdims=True),
     )):
         bounds_o[n * 16:(n + 1) * 16, :] = jnp.broadcast_to(v, (16, HS))
 
@@ -336,6 +344,7 @@
     anyspace = pl.BlockSpec(memory_space=pl.ANY)
     vmem = pl.BlockSpec(memory_space=pltpu.VMEM)
     dma = pltpu.SemaphoreType.DMA
+    hbm = pl.BlockSpec(memory_space=pltpu.HBM)
     return pl.pallas_call(
         front_kernel,
         out_shape=(
@@ -347,9 +356,11 @@
             jax.ShapeDtypeStruct((64, HS), jnp.int32),
             jax.ShapeDtypeStruct((NPACK, ROWS), BF),
         ),
-        in_specs=[pl.BlockSpec(memory_space=pltpu.SMEM), vmem, vmem] + [anyspace] * 4,
+        in_specs=[hbm, hbm, vmem] + [anyspace] * 4,
         out_specs=(anyspace, anyspace, vmem, vmem, vmem, vmem, vmem),
         scratch_shapes=[
+            pltpu.SMEM((4, 4), jnp.int32),
+            pltpu.VMEM((1, ROWS), jnp.int32),
             pltpu.VMEM((ROWS, HS), F32),
             pltpu.VMEM((ROWS, HS), F32),
             pltpu.VMEM((ROWS, D), BF),
@@ -366,7 +377,7 @@
             pltpu.VMEM((NPACK, QW), BF),
             pltpu.VMEM((NPACK, QW), BF),
             dma((3, KPARTS)), dma((4,)), dma((3,)), dma((1,)), dma((31,)), dma((1,)),
-            dma((3, 7)), dma((3,)), dma((30,)), dma((32,)), dma((32,)), dma((2,)), dma((2,)),
+            dma((3, 7)), dma((3,)), dma((30,)), dma((32,)), dma((32,)), dma((2,)), dma((2,)), dma((2,)),
         ],
         compiler_params=pltpu.CompilerParams(
             collective_id=0, has_side_effects=True, vmem_limit_bytes=47 << 20),
@@ -375,7 +386,7 @@
 
 
 def attend_kernel(
-    bounds, lanes, qsort, one, k_v, vt_v, out, osort, s_a, s_b, acc,
+    bounds, lanes, qsort, one, k_v, vt_v, out, osort, s_a, acc,
 ):
     osort[...] = jnp.zeros_like(osort)
     scale = math.log2(math.e) / math.sqrt(HS)
@@ -394,48 +405,47 @@
             half = lanes[pl.ds(n + 16, 1), :]
             begin = jnp.concatenate([half, half], axis=1)
 
-            def scores(t, ref):
-                keys = k_v[t]
-                ref[...] = lax.dot_general(
+            count = (high // ROWS - low // ROWS + 4) // 4
+            first = jnp.maximum(high // ROWS + 1 - 4 * count, 0)
+            origin = first * ROWS
+            full_from = jnp.clip((start_max - origin + KT - 1) // KT - 1, 0, count - 1)
+            full_to = jnp.clip((slot_min + 1 - origin) // KT - 1, full_from, count - 1)
+            acc[...] = jnp.zeros_like(acc)
+
+            def scores(masked, t):
+                keys = k_v[pl.ds(first + 4 * t, 4)].reshape(KT, HS)
+                s = scale * lax.dot_general(
                     keys, queries, (((1,), (1,)), ((), ())), preferred_element_type=F32)
-
-            first = low // KT
-            last = high // KT + 1
-            full_from = jnp.clip((start_max + KT - 1) // KT, first, last)
-            full_to = jnp.clip((slot_min + 1) // KT, full_from, last)
-            scores(2 * first, s_a)
-            scores(2 * first + 1, s_b)
-            acc[...] = jnp.zeros_like(acc)
+                if masked:
+                    at = lax.broadcasted_iota(jnp.int32, (KT, wide), 0)
+                    base = origin + t * KT
+                    s = jnp.where((at >= begin - base) & (at <= mine - base), s, -1e30)
+                return s, jnp.max(s, axis=0, keepdims=True)
+
+            def weigh(t, state):
+                top, total, peak = state
+                new = jnp.maximum(top, peak)
+                p = jnp.exp2(s_a[...] - new)
+                factor = jnp.exp2(top - new)
+                total = total * factor + jnp.sum(p, axis=0, keepdims=True)
+                values = jnp.concatenate([vt_v[first + 4 * t + u] for u in range(4)], axis=1)
+                acc[...] = acc[...] * factor + jnp.dot(
+                    values, p.astype(BF), preferred_element_type=F32)
+                return new, total
 
             def tile(masked, t, state):
-                top, total = state
-                a = s_a[...]
-                b = s_b[...]
-                if masked:
-                    at = lax.broadcasted_iota(jnp.int32, (ROWS, wide), 0)
-                    begin_a, mine_a = begin - t * KT, mine - t * KT
-                    begin_b, mine_b = begin_a - ROWS, mine_a - ROWS
-                    a = jnp.where((at >= begin_a) & (at <= mine_a), a, -1e30)
-                    b = jnp.where((at >= begin_b) & (at <= mine_b), b, -1e30)
-                new = jnp.maximum(
-                    top, jnp.max(jnp.maximum(a, b), axis=0, keepdims=True))
-                shift = new * scale
-                pa = jnp.exp2(a * scale - shift)
-                pb = jnp.exp2(b * scale - shift)
-                factor = jnp.exp2(top * scale - shift)
-                total = total * factor + jnp.sum(pa + pb, axis=0, keepdims=True)
-                after = jnp.minimum(t + 1, NBLOCKS // 2 - 1)
-                scores(2 * after, s_a)
-                scores(2 * after + 1, s_b)
-                acc[...] = acc[...] * factor + (
-                    jnp.dot(vt_v[2 * t], pa.astype(BF), preferred_element_type=F32)
-                    + jnp.dot(vt_v[2 * t + 1], pb.astype(BF), preferred_element_type=F32))
-                return new, total
-
-            state = (jnp.full((1, wide), -1e30, F32), jnp.zeros((1, wide), F32))
-            state = lax.fori_loop(first, full_from, functools.partial(tile, True), state)
+                s, peak = scores(masked, t + 1)
+                new, total = weigh(t, state)
+                s_a[...] = s
+                return new, total, peak
+
+            s, peak = scores(True, 0)
+            s_a[...] = s
+            state = (jnp.full((1, wide), -1e30, F32), jnp.zeros((1, wide), F32), peak)
+            state = lax.fori_loop(0, full_from, functools.partial(tile, True), state)
             state = lax.fori_loop(full_from, full_to, functools.partial(tile, False), state)
-            top, total = lax.fori_loop(full_to, last, functools.partial(tile, True), state)
+            state = lax.fori_loop(full_to, count - 1, functools.partial(tile, True), state)
+            top, total = weigh(count - 1, state)
             o = jnp.transpose(acc[...] / total).astype(BF)
             for h in range(HQ):
                 osort[rows, h * HS:(h + 1) * HS] = o[h * CHUNK:(h + 1) * CHUNK, :]
@@ -457,8 +467,7 @@
         out_specs=vmem,
         scratch_shapes=[
             pltpu.VMEM((NPACK, HQ * HS), BF),
-            pltpu.VMEM((ROWS, wide), F32),
-            pltpu.VMEM((ROWS, wide), F32),
+            pltpu.VMEM((KT, wide), F32),
             pltpu.VMEM((HS, wide), F32),
         ],
         compiler_params=pltpu.CompilerParams(vmem_limit_bytes=16 << 20),

time: 80.8 us -> 71.9 us (0.89)
  Pallas kernels: 79.2 us -> 70.3 us
    pallas_call x1, Pallas kernels: 20.8 us -> 13.7 us  [attend(): pl.pallas_call(attend_kernel, out_shape=jax.ShapeDtypeStruct((NPACK, HQ *...]
    pallas_call x1, Pallas kernels: 13.6 us -> 12.6 us  [back(): pl.pallas_call(back_kernel, out_shape=jax.ShapeDtypeStruct((NPACK, HQ * H...]
where the time goes in v4:
time: 71.9 us; the launch traced here: 71.7 us
  Pallas kernels  70.3 us (98%)
  local copies, waits for them, and re-layouts  1.36 us (2%)
    pallas_call x1, Pallas kernels, front(): pl.pallas_call(front_kernel, out_shape=(jax.ShapeDtypeStruct((NBLOCKS, RO...  42.8 us
    pallas_call x1, Pallas kernels, attend(): pl.pallas_call(attend_kernel, out_shape=jax.ShapeDtypeStruct((NPACK, HQ *...  13.7 us
    pallas_call x1, Pallas kernels, back(): pl.pallas_call(back_kernel, out_shape=jax.ShapeDtypeStruct((NPACK, HQ * H...  12.6 us

profile of v4, /device:TPU:1, one launch (start us, length us, event | category | flops | bytes accessed | tf_op | source)
XLA Modules:
  0.0 71.7 jit_solution(1729910225080519203)
XLA Ops:
  0.0 0.1 maximum_bitcast_fusion.freq
  0.1 0.0 copy-start
  0.1 0.7 copy-done
  0.8 0.0 copy-start.1
  0.8 0.7 copy-done.1
  1.5 42.8 %front.1 = (bf16[32,256,128]{2,1,0:T(8,128)(2,1)S(1)}, bf16[32,128,256]{2,1,0:T(8,128)(2,1)S(1)}, bf16[384,1024]{1,0:T(8,128)(2,1)S(1)}, bf16[384,384]{1,0:T(8,1...) custom-call(s32[4,4]{1,0:T(4,128)S(1)} %copy-done, ...), custom_call_target="tpu_custom_call" | custom-call | tf_op jit(solution)/shard_map/front/pallas_call | solution.py:348
  44.2 13.7 %attend.1.packed = bf16[384,1024]{1,0:T(8,128)(2,1)S(1)} custom-call(s32[64,128]{1,0:T(8,128)S(1)} %get-tuple-element.13.bounds, s32[32,128]{1,0:T(8,128)S(1)} %get-tuple-element.14.lanes, bf16[384,1024]{1,0:T(8,128)(2,1)S(1)} %get-tuple-element.15.qsort, bf16[384,384]{1,0:T(8,128)(2,1)S(1)} %get-tuple-element.16.one, ...), custom_call_target="tpu_custom_call" | custom-call | tf_op jit(solution)/shard_map/attend/pallas_call | solution.py:463
  57.9 12.6 %back.1.ret = bf16[384,1024]{1,0:T(8,128)(2,1)S(1)} custom-call(bf16[384,1024]{1,0:T(8,128)(2,1)S(1)} %attend.1.packed), custom_call_target="tpu_custom_call" | custom-call | tf_op jit(solution)/shard_map/back/pallas_call | solution.py:507
  70.5 1.3 %finish.1 = bf16[256,1024]{1,0:T(8,128)(2,1)} custom-call(bf16[384,256]{1,0:T(8,128)(2,1)S(1)} %get-tuple-element.12.pack, bf16[384,1024]{1,0:T(8,128)(2,1)S(1)} %back.1.ret), custom_call_target="tpu_custom_call" | custom-call | tf_op jit(solution)/shard_map/finish/pallas_call | solution.py:524
  (1 shorter events, 0.0 us)
Async XLA Ops:
  0.1 0.7 copy-start
  0.8 0.7 copy-start.1

commit v5 on v4

--- a/solution.py
+++ b/solution.py
@@ -52,23 +52,26 @@
 
 
 def front_kernel(
-    lengths_ref, slot_hbm, freq, tok, wq, wk, wv,
+    ints, freq, tok, wq, wk, wv,
     kall, vtall, qsort, one_o, lanes_o, bounds_o, pack_o,
-    lengths, slot_ref, cos, sin, tok_v, wkv_v, wq_v, acc, kvs, zin, perm, aout, ain, kblk, vblk, qs, qin,
+    lengths, cos, sin, tok_v, wkv_v, wq_v, acc, kvs, zin, perm, aout, ain, kblk, vblk, qs, qin,
     tok_sem, wq_sem, zs_sem, zr_sem, as_sem, ar_sem, qs_sem, qr_sem,
-    ts_sem, tr_sem, ds_sem, dr_sem, loc_sem, small_sem,
+    ts_sem, tr_sem, dr_sem, loc_sem, small_sem,
 ):
     x, y, z, c = place()
+    xs, ys, zs = ([v if n == 0 else (v + n) % 4 for n in range(4)] for v in (x, y, z))
+    low, high = [v % 2 * 2 for v in ys], [v // 2 * 4 for v in ys]
+    cs = [c, 1 - c]
     kc = D // KPARTS
     mine = block_id(x, y, c)
+
+    def at(dx, dy, dz, dc):
+        return low[dy] + cs[dc], xs[dx] * 8 + high[dy] + zs[dz]
+
     line = z * 2 + c
 
-    small = [
-        pltpu.make_async_copy(lengths_ref, lengths, small_sem.at[0]),
-        pltpu.make_async_copy(slot_hbm, slot_ref, small_sem.at[1]),
-    ]
-    for load in small:
-        load.start()
+    small = pltpu.make_async_copy(ints, lengths, small_sem.at[0])
+    small.start()
     loads = []
     for i in range(KPARTS):
         part = pl.ds(i * kc, kc)
@@ -84,26 +87,15 @@
         cols = pl.ds(n * 256, 256)
         qloads.append(pltpu.make_async_copy(wq.at[:, cols], wq_v.at[n], wq_sem.at[n]))
 
-    peers = []
-    for dz in range(4):
-        for dc in range(2):
-            if (dz, dc) != (0, 0):
-                peers.append(((z + dz) % 4, (c + dc) % 2))
-    flat = []
-    for dx in range(4):
-        for dy in range(4):
-            for dc in range(2):
-                if (dx, dy, dc) != (0, 0, 0):
-                    flat.append(((x + dx) % 4, (y + dy) % 4, (c + dc) % 2))
+    peers = [(dz, dc) for dz in range(4) for dc in range(2)][1:]
+    flat = [(dx, dy, dc) for dx in range(4) for dy in range(4) for dc in range(2)][1:]
     barrier = pltpu.get_barrier_semaphore()
-    for pz, pc in peers:
-        pl.semaphore_signal(barrier, inc=1, device_id=device(x, y, pz, pc), device_id_type=MESH)
-    for px, py, pc in flat:
-        pl.semaphore_signal(barrier, inc=1, device_id=device(px, py, z, pc), device_id_type=MESH)
-
-    for load in small:
-        load.wait()
-    slot_r = slot_ref[...]
+    for dz, dc in peers:
+        pl.semaphore_signal(barrier, inc=1, device_id=at(0, 0, dz, dc), device_id_type=MESH)
+    for dx, dy, dc in flat:
+        pl.semaphore_signal(barrier, inc=1, device_id=at(dx, dy, 0, dc), device_id_type=MESH)
+
+    slot_r = ints[0:1, :]
     block_r = slot_r >> 8
     slot_c = jnp.transpose(jnp.broadcast_to(slot_r.astype(F32), (HS, ROWS))).astype(jnp.int32)
     block_c = slot_c >> 8
@@ -119,18 +111,24 @@
     slots = jnp.dot(pack, meta, preferred_element_type=F32).astype(BF)
     kvs[:, 2 * HS:] = slots
     qs[:, 0:128] = slots
+    small.wait()
     local_c = slot_c & 8191
     group_c = slot_c >> 13
     start_c = jnp.zeros_like(slot_c)
     for g in range(4):
         end = 0
         for d in range(3):
-            end = end + lengths[g, d]
+            end = end + lengths[1 + g, d]
             start_c = jnp.where((group_c == g) & (local_c >= end), end, start_c)
     angle = (local_c - start_c).astype(F32) * freq[...]
-    cos[...] = jnp.cos(angle)
-    sine = jnp.sin(angle)
-    sin[...] = jnp.where(lax.broadcasted_iota(jnp.int32, (ROWS, HS), 1) < HS // 2, -sine, sine)
+    left = lax.broadcasted_iota(jnp.int32, (HS, HS), 1) < HS // 2
+    angle = jnp.where(left, angle[:HS], angle[HS:])
+    cosine, sine = jnp.cos(angle), jnp.sin(angle)
+    cosine_r, sine_r = pltpu.roll(cosine, HS // 2, 1), pltpu.roll(sine, HS // 2, 1)
+    cos[0:HS, :] = jnp.where(left, cosine, cosine_r)
+    cos[HS:, :] = jnp.where(left, cosine_r, cosine)
+    sin[0:HS, :] = jnp.where(left, -sine, sine_r)
+    sin[HS:, :] = jnp.where(left, -sine_r, sine)
 
     for i in range(KPARTS):
         part = pl.ds(i * kc, kc)
@@ -150,37 +148,34 @@
 
     pl.semaphore_wait(barrier, 7 + 31)
 
-    sends = []
     for dz in range(1, 4):
-        pz = (z + dz) % 4
-        sends.append(pltpu.make_async_remote_copy(
-            src_ref=kvs.at[pl.ds(pz * 96, 96), :], dst_ref=zin.at[pl.ds(z * 96, 96), :],
-            send_sem=zs_sem.at[dz - 1], recv_sem=zr_sem.at[0],
-            device_id=device(x, y, pz, c), device_id_type=MESH))
-        sends[-1].start()
+        pltpu.make_async_remote_copy(
+            src_ref=kvs.at[pl.ds(zs[dz] * 96, 96), :], dst_ref=zin.at[pl.ds(z * 96, 96), :],
+            send_sem=zs_sem.at[0], recv_sem=zr_sem.at[0],
+            device_id=at(0, 0, dz, 0), device_id_type=MESH).start()
     pltpu.make_async_copy(
         kvs.at[pl.ds(z * 96, 96), :], zin.at[pl.ds(z * 96, 96), :], zr_sem.at[0]).start()
 
+    columns = (pl.ds(0, 128), pl.ds(128, 512), pl.ds(640, 512))
+
     def query_send(part):
-        cols = (pl.ds(0, 128), pl.ds(128, 512), pl.ds(640, 512))[part]
-        for i, (pz, pc) in enumerate(peers):
-            sends.append(pltpu.make_async_remote_copy(
-                src_ref=qs.at[pl.ds((pz * 2 + pc) * PACK, PACK), cols],
+        cols = columns[part]
+        for dz, dc in peers:
+            pltpu.make_async_remote_copy(
+                src_ref=qs.at[pl.ds((zs[dz] * 2 + cs[dc]) * PACK, PACK), cols],
                 dst_ref=qin.at[pl.ds(line * PACK, PACK), cols],
-                send_sem=qs_sem.at[part, i], recv_sem=qr_sem.at[part],
-                device_id=device(x, y, pz, pc), device_id_type=MESH))
-            sends[-1].start()
+                send_sem=qs_sem.at[part], recv_sem=qr_sem.at[part],
+                device_id=at(0, 0, dz, dc), device_id_type=MESH).start()
         pltpu.make_async_copy(
             qs.at[pl.ds(line * PACK, PACK), cols], qin.at[pl.ds(line * PACK, PACK), cols],
             qr_sem.at[part]).start()
 
     def query_wait(part):
-        cols = (pl.ds(0, 128), pl.ds(128, 512), pl.ds(640, 512))[part]
+        cols = columns[part]
         pltpu.make_async_copy(qin.at[:, cols], qin.at[:, cols], qr_sem.at[part]).wait()
 
-    def flush():
-        while sends:
-            sends.pop(0).wait_send()
+    def sent(ref, sem):
+        pltpu.make_async_copy(ref, ref, sem).wait()
 
     query_send(0)
 
@@ -210,13 +205,12 @@
 
     pltpu.make_async_copy(zin, zin, zr_sem.at[0]).wait()
     aout[...] = jnp.dot(perm[...], zin[...], preferred_element_type=F32).astype(BF)
-    for i, (px, py, pc) in enumerate(flat):
-        sends.append(pltpu.make_async_remote_copy(
-            src_ref=aout.at[pl.ds(block_id(px, py, pc) * 16, 16), :],
+    for dx, dy, dc in flat:
+        pltpu.make_async_remote_copy(
+            src_ref=aout.at[pl.ds(block_id(xs[dx], ys[dy], cs[dc]) * 16, 16), :],
             dst_ref=ain.at[pl.ds(mine * 16, 16), :],
-            send_sem=as_sem.at[i], recv_sem=ar_sem.at[0],
-            device_id=device(px, py, z, pc), device_id_type=MESH))
-        sends[-1].start()
+            send_sem=as_sem.at[0], recv_sem=ar_sem.at[0],
+            device_id=at(dx, dy, 0, dc), device_id_type=MESH).start()
     pltpu.make_async_copy(
         aout.at[pl.ds(mine * 16, 16), :], ain.at[pl.ds(mine * 16, 16), :], ar_sem.at[0]).start()
 
@@ -247,7 +241,7 @@
     start = jnp.zeros_like(slots)
     end = 0
     for d in range(3):
-        end = end + lengths[z, d]
+        end = end + lengths[1 + z, d]
         start = jnp.where(slots >= end, end, start)
     lanes_o[16:32, :] = start
     for n, v in enumerate((
@@ -269,35 +263,37 @@
     kblk[...] = dot_t(one, ain[:, 0:HS]).astype(BF)
     vblk[...] = dot_t(ain[:, HS:2 * HS], one).astype(BF)
 
-    def at_offset(a, b):
-        return (x + a * (1 - c) + b * c) % 4, (y + a * c + b * (1 - c)) % 4
+    blocks = [[
+        (xs[a] + (xs[b] - xs[a]) * c) * 4 + ys[b] + (ys[a] - ys[b]) * c + 16 * c
+        for b in range(4)] for a in range(4)]
+
+    def along(a, b):
+        one, two = at(a, b, 0, 0), at(b, a, 0, 0)
+        return tuple(u + (v - u) * c for u, v in zip(one, two))
+
+    first, second = [None] + [along(n, 0) for n in (1, 2, 3)], [None] + [along(0, n) for n in (1, 2, 3)]
 
     def piece(q, a, b):
-        px, py = at_offset(a, b)
-        return (kall if q == 0 else vtall).at[block_id(px, py, c)]
+        return (kall if q == 0 else vtall).at[blocks[a][b]]
 
     def source_of(q, a, b):
         if (a, b) == (0, 0):
             return kblk if q == 0 else vblk
         return piece(q, a, b)
 
-    count = [0]
-
     def push(q, a, b, da, db):
-        px, py = at_offset(da, db)
-        sends.append(pltpu.make_async_remote_copy(
+        pltpu.make_async_remote_copy(
             src_ref=source_of(q, a, b), dst_ref=piece(q, a, b),
-            send_sem=ts_sem.at[count[0]], recv_sem=tr_sem.at[q * 16 + (a - da) % 4 * 4 + (b - db) % 4],
-            device_id=device(px, py, z, c), device_id_type=MESH))
-        sends[-1].start()
-        count[0] += 1
+            send_sem=ts_sem.at[q], recv_sem=tr_sem.at[q * 16 + (a - da) % 4 * 4 + (b - db) % 4],
+            device_id=first[da] if db == 0 else second[db], device_id_type=MESH).start()
+
+    partner = at(0, 0, 0, 1)
 
     def share(q, a, b):
-        sends.append(pltpu.make_async_remote_copy(
+        pltpu.make_async_remote_copy(
             src_ref=source_of(q, a, b), dst_ref=piece(q, a, b),
-            send_sem=ds_sem.at[q * 16 + a * 4 + b], recv_sem=dr_sem.at[q],
-            device_id=device(x, y, z, 1 - c), device_id_type=MESH))
-        sends[-1].start()
+            send_sem=ts_sem.at[q], recv_sem=dr_sem.at[q],
+            device_id=partner, device_id_type=MESH).start()
 
     local = [
         pltpu.make_async_copy(source_of(q, 0, 0), piece(q, 0, 0), loc_sem.at[q]) for q in range(2)]
@@ -327,8 +323,10 @@
     query_wait(1)
     query_wait(2)
     qsort[...] = dot_t(one_o[...], qin[:, HS:]).astype(BF)
-    while len(sends) > 36:
-        sends.pop(0).wait_send()
+    sent(zin.at[pl.ds(0, 288), :], zs_sem.at[0])
+    sent(aout.at[pl.ds(0, 31 * 16), :], as_sem.at[0])
+    for n, cols in enumerate(columns):
+        sent(qs.at[pl.ds(0, 7 * PACK), cols], qs_sem.at[n])
     for a, b in ((0, 2), (1, 2), (3, 2), (2, 2)):
         for q in range(2):
             arrive(q, a, b)
@@ -337,14 +335,14 @@
     pltpu.make_async_copy(vtall.at[other], vtall.at[other], dr_sem.at[1]).wait()
     for copy in local:
         copy.wait()
-    flush()
-
-
-def front(lengths, slot_row, freq, tokens, wq, wk, wv):
+    sent(kall.at[pl.ds(0, 31)], ts_sem.at[0])
+    sent(vtall.at[pl.ds(0, 31)], ts_sem.at[1])
+
+
+def front(ints, freq, tokens, wq, wk, wv):
     anyspace = pl.BlockSpec(memory_space=pl.ANY)
     vmem = pl.BlockSpec(memory_space=pltpu.VMEM)
     dma = pltpu.SemaphoreType.DMA
-    hbm = pl.BlockSpec(memory_space=pltpu.HBM)
     return pl.pallas_call(
         front_kernel,
         out_shape=(
@@ -356,11 +354,10 @@
             jax.ShapeDtypeStruct((64, HS), jnp.int32),
             jax.ShapeDtypeStruct((NPACK, ROWS), BF),
         ),
-        in_specs=[hbm, hbm, vmem] + [anyspace] * 4,
+        in_specs=[vmem, vmem] + [anyspace] * 4,
         out_specs=(anyspace, anyspace, vmem, vmem, vmem, vmem, vmem),
         scratch_shapes=[
-            pltpu.SMEM((4, 4), jnp.int32),
-            pltpu.VMEM((1, ROWS), jnp.int32),
+            pltpu.SMEM((8, ROWS), jnp.int32),
             pltpu.VMEM((ROWS, HS), F32),
             pltpu.VMEM((ROWS, HS), F32),
             pltpu.VMEM((ROWS, D), BF),
@@ -376,13 +373,13 @@
             pltpu.VMEM((HS, ROWS), BF),
             pltpu.VMEM((NPACK, QW), BF),
             pltpu.VMEM((NPACK, QW), BF),
-            dma((3, KPARTS)), dma((4,)), dma((3,)), dma((1,)), dma((31,)), dma((1,)),
-            dma((3, 7)), dma((3,)), dma((30,)), dma((32,)), dma((32,)), dma((2,)), dma((2,)), dma((2,)),
+            dma((3, KPARTS)), dma((4,)), dma((1,)), dma((1,)), dma((1,)), dma((1,)),
+            dma((3,)), dma((3,)), dma((2,)), dma((32,)), dma((2,)), dma((2,)), dma((1,)),
         ],
         compiler_params=pltpu.CompilerParams(
             collective_id=0, has_side_effects=True, vmem_limit_bytes=47 << 20),
         name="front",
-    )(lengths, slot_row, freq, tokens, wq, wk, wv)
+    )(ints, freq, tokens, wq, wk, wv)
 
 
 def attend_kernel(
@@ -482,24 +479,22 @@
     for dz in range(4):
         for dc in range(2):
             if (dz, dc) != (0, 0):
-                peers.append(((z + dz) % 4, (c + dc) % 2))
+                peers.append(((z + dz) % 4, c if dc == 0 else 1 - c))
     barrier = pltpu.get_barrier_semaphore()
     for pz, pc in peers:
         pl.semaphore_signal(barrier, inc=1, device_id=device(x, y, pz, pc), device_id_type=MESH)
     pl.semaphore_wait(barrier, 7)
-    sends = []
-    for i, (pz, pc) in enumerate(peers):
-        sends.append(pltpu.make_async_remote_copy(
+    for pz, pc in peers:
+        pltpu.make_async_remote_copy(
             src_ref=packed.at[pl.ds((pz * 2 + pc) * PACK, PACK), :],
             dst_ref=ret.at[pl.ds(line * PACK, PACK), :],
-            send_sem=send_sem.at[i], recv_sem=recv_sem.at[0],
-            device_id=device(x, y, pz, pc), device_id_type=MESH))
-        sends[-1].start()
+            send_sem=send_sem.at[0], recv_sem=recv_sem.at[0],
+            device_id=device(x, y, pz, pc), device_id_type=MESH).start()
     pltpu.make_async_copy(
         packed.at[pl.ds(line * PACK, PACK), :], ret.at[pl.ds(line * PACK, PACK), :], recv_sem.at[0]).start()
     pltpu.make_async_copy(ret, ret, recv_sem.at[0]).wait()
-    for copy in sends:
-        copy.wait_send()
+    part = packed.at[pl.ds(0, 7 * PACK), :]
+    pltpu.make_async_copy(part, part, send_sem.at[0]).wait()
 
 
 def back(packed):
@@ -509,7 +504,7 @@
         out_shape=jax.ShapeDtypeStruct((NPACK, HQ * HS), BF),
         in_specs=[vmem],
         out_specs=pl.BlockSpec(memory_space=pl.ANY),
-        scratch_shapes=[pltpu.SemaphoreType.DMA((7,)), pltpu.SemaphoreType.DMA((1,))],
+        scratch_shapes=[pltpu.SemaphoreType.DMA((1,)), pltpu.SemaphoreType.DMA((1,))],
         compiler_params=pltpu.CompilerParams(collective_id=1, has_side_effects=True, vmem_limit_bytes=4 << 20),
         name="back",
     )(packed)
@@ -534,8 +529,9 @@
 def shards(tokens, query_weight, key_weight, value_weight, doc_lengths, slot_index):
     frequency = 500000.0 ** (-(jnp.arange(HS // 2, dtype=F32) * 2.0 / HS))
     frequency = jnp.concatenate([frequency, frequency])[None, :]
+    ints = jnp.concatenate([slot_index[None, :], jnp.pad(doc_lengths, ((0, 3), (0, ROWS - 4)))], axis=0)
     kall, vtall, qsort, one, lanes, bounds, pack = front(
-        doc_lengths, slot_index[None, :], frequency, tokens, query_weight, key_weight, value_weight)
+        ints, frequency, tokens, query_weight, key_weight, value_weight)
     packed = attend(bounds, lanes, qsort, one, kall, vtall)
     return finish(pack, back(packed))
 

time: 71.9 us -> 70.6 us (0.982)
  the two profiles are of different devices: /device:TPU:1 before, /device:TPU:7 now
where the time goes in v5:
time: 70.6 us; the launch traced here: 70.9 us
  Pallas kernels  70 us (99%)
  other arithmetic  0.8 us (1%)
    pallas_call x1, Pallas kernels, front(): pl.pallas_call(front_kernel, out_shape=(jax.ShapeDtypeStruct((NBLOCKS, RO...  41 us
    pallas_call x1, Pallas kernels, attend(): pl.pallas_call(attend_kernel, out_shape=jax.ShapeDtypeStruct((NPACK, HQ *...  14.4 us
    pallas_call x1, Pallas kernels, back(): pl.pallas_call(back_kernel, out_shape=jax.ShapeDtypeStruct((NPACK, HQ * H...  13.4 us

profile of v5, /device:TPU:7, one launch (start us, length us, event | category | flops | bytes accessed | tf_op | source)
XLA Modules:
  0.0 70.9 jit_solution(2308762917237733158)
XLA Ops:
  0.0 0.1 maximum_bitcast_fusion.freq
  0.1 0.7 pad_add_fusion.ints
  0.8 41.0 %front.1 = (bf16[32,256,128]{2,1,0:T(8,128)(2,1)S(1)}, bf16[32,128,256]{2,1,0:T(8,128)(2,1)S(1)}, bf16[384,1024]{1,0:T(8,128)(2,1)S(1)}, bf16[384,384]{1,0:T(8,1...) custom-call(s32[8,256]{1,0:T(8,128)S(1)} %pad_add_fusion.ints, ...), custom_call_target="tpu_custom_call" | custom-call | tf_op jit(solution)/shard_map/front/pallas_call | solution.py:346
  41.8 14.4 %attend.1.packed = bf16[384,1024]{1,0:T(8,128)(2,1)S(1)} custom-call(s32[64,128]{1,0:T(8,128)S(1)} %get-tuple-element.13.bounds, s32[32,128]{1,0:T(8,128)S(1)} %get-tuple-element.14.lanes, bf16[384,1024]{1,0:T(8,128)(2,1)S(1)} %get-tuple-element.15.qsort, bf16[384,384]{1,0:T(8,128)(2,1)S(1)} %get-tuple-element.16.one, ...), custom_call_target="tpu_custom_call" | custom-call | tf_op jit(solution)/shard_map/attend/pallas_call | solution.py:460
  56.2 13.4 %back.1.ret = bf16[384,1024]{1,0:T(8,128)(2,1)S(1)} custom-call(bf16[384,1024]{1,0:T(8,128)(2,1)S(1)} %attend.1.packed), custom_call_target="tpu_custom_call" | custom-call | tf_op jit(solution)/shard_map/back/pallas_call | solution.py:502
  69.6 1.3 %finish.1 = bf16[256,1024]{1,0:T(8,128)(2,1)} custom-call(bf16[384,256]{1,0:T(8,128)(2,1)S(1)} %get-tuple-element.12.pack, bf16[384,1024]{1,0:T(8,128)(2,1)S(1)} %back.1.ret), custom_call_target="tpu_custom_call" | custom-call | tf_op jit(solution)/shard_map/finish/pallas_call | solution.py:519
  (1 shorter events, 0.0 us)

commit v6 on v5

--- a/solution.py
+++ b/solution.py
@@ -17,7 +17,7 @@
 PACK = 48
 NPACK = 8 * PACK
 QW = 128 + HQ * HS
-KT = 1024
+TILES = (3, 4, 5, 6, 8)
 KPARTS = 8
 CHUNK = 32
 NCHUNK = NPACK // CHUNK
@@ -89,6 +89,7 @@
 
     peers = [(dz, dc) for dz in range(4) for dc in range(2)][1:]
     flat = [(dx, dy, dc) for dx in range(4) for dy in range(4) for dc in range(2)][1:]
+    flat.sort(key=lambda o: -(min(o[0], 4 - o[0]) + min(o[1], 4 - o[1])))
     barrier = pltpu.get_barrier_semaphore()
     for dz, dc in peers:
         pl.semaphore_signal(barrier, inc=1, device_id=at(0, 0, dz, dc), device_id_type=MESH)
@@ -148,7 +149,7 @@
 
     pl.semaphore_wait(barrier, 7 + 31)
 
-    for dz in range(1, 4):
+    for dz in (2, 1, 3):
         pltpu.make_async_remote_copy(
             src_ref=kvs.at[pl.ds(zs[dz] * 96, 96), :], dst_ref=zin.at[pl.ds(z * 96, 96), :],
             send_sem=zs_sem.at[0], recv_sem=zr_sem.at[0],
@@ -383,14 +384,14 @@
 
 
 def attend_kernel(
-    bounds, lanes, qsort, one, k_v, vt_v, out, osort, s_a, acc,
+    bounds, lanes, qsort, one, k_v, vt_v, out, osort, s_a, acc, total_s,
 ):
     osort[...] = jnp.zeros_like(osort)
     scale = math.log2(math.e) / math.sqrt(HS)
     wide = CHUNK * HQ
 
     def chunk(n, carry):
-        low, high, start_max, slot_min = (bounds[16 * v + n, 0] for v in range(4))
+        low, high = bounds[n, 0], bounds[16 + n, 0]
 
         @pl.when(high >= 0)
         def _():
@@ -402,47 +403,59 @@
             half = lanes[pl.ds(n + 16, 1), :]
             begin = jnp.concatenate([half, half], axis=1)
 
-            count = (high // ROWS - low // ROWS + 4) // 4
-            first = jnp.maximum(high // ROWS + 1 - 4 * count, 0)
-            origin = first * ROWS
-            full_from = jnp.clip((start_max - origin + KT - 1) // KT - 1, 0, count - 1)
-            full_to = jnp.clip((slot_min + 1 - origin) // KT - 1, full_from, count - 1)
+            spans = high // ROWS - low // ROWS + 1
+            counts = [(spans + nb - 1) // nb for nb in TILES]
+            prices = [
+                jnp.where(n * nb <= NBLOCKS, n * (174 + 62 * nb), 1 << 20)
+                for n, nb in zip(counts, TILES)]
+            best = functools.reduce(jnp.minimum, prices)
             acc[...] = jnp.zeros_like(acc)
 
-            def scores(masked, t):
-                keys = k_v[pl.ds(first + 4 * t, 4)].reshape(KT, HS)
-                s = scale * lax.dot_general(
-                    keys, queries, (((1,), (1,)), ((), ())), preferred_element_type=F32)
-                if masked:
-                    at = lax.broadcasted_iota(jnp.int32, (KT, wide), 0)
-                    base = origin + t * KT
-                    s = jnp.where((at >= begin - base) & (at <= mine - base), s, -1e30)
-                return s, jnp.max(s, axis=0, keepdims=True)
-
-            def weigh(t, state):
-                top, total, peak = state
-                new = jnp.maximum(top, peak)
-                p = jnp.exp2(s_a[...] - new)
-                factor = jnp.exp2(top - new)
-                total = total * factor + jnp.sum(p, axis=0, keepdims=True)
-                values = jnp.concatenate([vt_v[first + 4 * t + u] for u in range(4)], axis=1)
-                acc[...] = acc[...] * factor + jnp.dot(
-                    values, p.astype(BF), preferred_element_type=F32)
-                return new, total
-
-            def tile(masked, t, state):
-                s, peak = scores(masked, t + 1)
-                new, total = weigh(t, state)
-                s_a[...] = s
-                return new, total, peak
-
-            s, peak = scores(True, 0)
-            s_a[...] = s
-            state = (jnp.full((1, wide), -1e30, F32), jnp.zeros((1, wide), F32), peak)
-            state = lax.fori_loop(0, full_from, functools.partial(tile, True), state)
-            state = lax.fori_loop(full_from, full_to, functools.partial(tile, False), state)
-            state = lax.fori_loop(full_to, count - 1, functools.partial(tile, True), state)
-            top, total = weigh(count - 1, state)
+            def run(nb, count):
+                kt = nb * ROWS
+                first = jnp.maximum(high // ROWS + 1 - nb * count, 0)
+                origin = first * ROWS
+                part = s_a.at[pl.ds(0, kt), :]
+
+                def scores(t):
+                    keys = k_v[pl.ds(first + nb * t, nb)].reshape(kt, HS)
+                    s = scale * lax.dot_general(
+                        keys, queries, (((1,), (1,)), ((), ())), preferred_element_type=F32)
+                    at = lax.broadcasted_iota(jnp.int32, (kt, wide), 0)
+                    base = origin + t * kt
+                    past = (at - (begin - base)).astype(jnp.uint32)
+                    s = jnp.where(past <= (mine - begin).astype(jnp.uint32), s, -1e30)
+                    return s, jnp.max(s, axis=0, keepdims=True)
+
+                def weigh(t, state):
+                    top, total, peak = state
+                    new = jnp.maximum(top, peak)
+                    p = jnp.exp2(part[...] - new)
+                    factor = jnp.exp2(top - new)
+                    total = total * factor + jnp.sum(p, axis=0, keepdims=True)
+                    values = jnp.concatenate([vt_v[first + nb * t + u] for u in range(nb)], axis=1)
+                    acc[...] = acc[...] * factor + jnp.dot(
+                        values, p.astype(BF), preferred_element_type=F32)
+                    return new, total
+
+                def tile(t, state):
+                    s, peak = scores(t + 1)
+                    new, total = weigh(t, state)
+                    part[...] = s
+                    return new, total, peak
+
+                s, peak = scores(0)
+                part[...] = s
+                state = (jnp.full((1, wide), -1e30, F32), jnp.zeros((1, wide), F32), peak)
+                state = lax.fori_loop(0, count - 1, tile, state)
+                total_s[...] = weigh(count - 1, state)[1]
+
+            taken = False
+            for nb, count, price in zip(TILES, counts, prices):
+                now = price == best
+                pl.when(jnp.logical_and(now, jnp.logical_not(taken)))(functools.partial(run, nb, count))
+                taken = jnp.logical_or(taken, now)
+            total = total_s[...]
             o = jnp.transpose(acc[...] / total).astype(BF)
             for h in range(HQ):
                 osort[rows, h * HS:(h + 1) * HS] = o[h * CHUNK:(h + 1) * CHUNK, :]
@@ -464,8 +477,9 @@
         out_specs=vmem,
         scratch_shapes=[
             pltpu.VMEM((NPACK, HQ * HS), BF),
-            pltpu.VMEM((KT, wide), F32),
+            pltpu.VMEM((TILES[-1] * ROWS, wide), F32),
             pltpu.VMEM((HS, wide), F32),
+            pltpu.VMEM((1, wide), F32),
         ],
         compiler_params=pltpu.CompilerParams(vmem_limit_bytes=16 << 20),
         name="attend",

time: 70.6 us -> 70.3 us (level)
  the two profiles are of different devices: /device:TPU:7 before, /device:TPU:1 now
where the time goes in v6:
time: 70.3 us; the launch traced here: 70.2 us
  Pallas kernels  69.4 us (99%)
  other arithmetic  0.8 us (1%)
    pallas_call x1, Pallas kernels, front(): pl.pallas_call(front_kernel, out_shape=(jax.ShapeDtypeStruct((NBLOCKS, RO...  41.4 us
    pallas_call x1, Pallas kernels, attend(): pl.pallas_call(attend_kernel, out_shape=jax.ShapeDtypeStruct((NPACK, HQ *...  13.6 us
    pallas_call x1, Pallas kernels, back(): pl.pallas_call(back_kernel, out_shape=jax.ShapeDtypeStruct((NPACK, HQ * H...  13.1 us

profile of v6, /device:TPU:1, one launch (start us, length us, event | category | flops | bytes accessed | tf_op | source)
XLA Modules:
  0.0 70.2 jit_solution(9911589887488288353)
XLA Ops:
  0.0 0.1 maximum_bitcast_fusion.freq
  0.1 0.7 %pad_add_fusion.ints = s32[8,256]{1,0:T(8,128)S(1)} fusion(s32[4,4]{1,0:T(4,128)} %param.10, s32[1,256]{1,0:T(1,128)} %bitcast.3), kind=kLoop, calls=%fused_computation | loop fusion | flops 2048 | bytes 9280 | tf_op jit(solution)/shard_map/concatenate | solution.py:546
  0.8 41.4 %front.1 = (bf16[32,256,128]{2,1,0:T(8,128)(2,1)S(1)}, bf16[32,128,256]{2,1,0:T(8,128)(2,1)S(1)}, bf16[384,1024]{1,0:T(8,128)(2,1)S(1)}, bf16[384,384]{1,0:T(8,1...) custom-call(s32[8,256]{1,0:T(8,128)S(1)} %pad_add_fusion.ints, ...), custom_call_target="tpu_custom_call" | custom-call | tf_op jit(solution)/shard_map/front/pallas_call | solution.py:347
  42.2 13.6 %attend.1.packed = bf16[384,1024]{1,0:T(8,128)(2,1)S(1)} custom-call(s32[64,128]{1,0:T(8,128)S(1)} %get-tuple-element.13.bounds, s32[32,128]{1,0:T(8,128)S(1)} %get-tuple-element.14.lanes, bf16[384,1024]{1,0:T(8,128)(2,1)S(1)} %get-tuple-element.15.qsort, bf16[384,384]{1,0:T(8,128)(2,1)S(1)} %get-tuple-element.16.one, ...), custom_call_target="tpu_custom_call" | custom-call | tf_op jit(solution)/shard_map/attend/pallas_call | solution.py:473
  55.8 13.1 %back.1.ret = bf16[384,1024]{1,0:T(8,128)(2,1)S(1)} custom-call(bf16[384,1024]{1,0:T(8,128)(2,1)S(1)} %attend.1.packed), custom_call_target="tpu_custom_call" | custom-call | tf_op jit(solution)/shard_map/back/pallas_call | solution.py:516
  68.9 1.3 %finish.1 = bf16[256,1024]{1,0:T(8,128)(2,1)} custom-call(bf16[384,256]{1,0:T(8,128)(2,1)S(1)} %get-tuple-element.12.pack, bf16[384,1024]{1,0:T(8,128)(2,1)S(1)} %back.1.ret), custom_call_target="tpu_custom_call" | custom-call | tf_op jit(solution)/shard_map/finish/pallas_call | solution.py:533
  (1 shorter events, 0.0 us)

commit v7 on v5

--- a/solution.py
+++ b/solution.py
@@ -416,7 +416,8 @@
                 if masked:
                     at = lax.broadcasted_iota(jnp.int32, (KT, wide), 0)
                     base = origin + t * KT
-                    s = jnp.where((at >= begin - base) & (at <= mine - base), s, -1e30)
+                    past = (at - (begin - base)).astype(jnp.uint32)
+                    s = jnp.where(past <= (mine - begin).astype(jnp.uint32), s, -1e30)
                 return s, jnp.max(s, axis=0, keepdims=True)
 
             def weigh(t, state):

time: 70.6 us -> 70.3 us (level)
  the two profiles are of different devices: /device:TPU:7 before, /device:TPU:1 now
where the time goes in v7:
time: 70.3 us; the launch traced here: 69.8 us
  Pallas kernels  69 us (98%)
  other arithmetic  0.8 us (1%)
    pallas_call x1, Pallas kernels, front(): pl.pallas_call(front_kernel, out_shape=(jax.ShapeDtypeStruct((NBLOCKS, RO...  41.7 us
    pallas_call x1, Pallas kernels, attend(): pl.pallas_call(attend_kernel, out_shape=jax.ShapeDtypeStruct((NPACK, HQ *...  13.5 us
    pallas_call x1, Pallas kernels, back(): pl.pallas_call(back_kernel, out_shape=jax.ShapeDtypeStruct((NPACK, HQ * H...  12.6 us

profile of v7, /device:TPU:1, one launch (start us, length us, event | category | flops | bytes accessed | tf_op | source)
XLA Modules:
  0.0 69.8 jit_solution(4732325449500934274)
XLA Ops:
  0.0 0.1 maximum_bitcast_fusion.freq
  0.1 0.7 %pad_add_fusion.ints = s32[8,256]{1,0:T(8,128)S(1)} fusion(s32[4,4]{1,0:T(4,128)} %param.10, s32[1,256]{1,0:T(1,128)} %bitcast.3), kind=kLoop, calls=%fused_computation | loop fusion | flops 2048 | bytes 9280 | tf_op jit(solution)/shard_map/concatenate | solution.py:533
  0.8 41.7 %front.1 = (bf16[32,256,128]{2,1,0:T(8,128)(2,1)S(1)}, bf16[32,128,256]{2,1,0:T(8,128)(2,1)S(1)}, bf16[384,1024]{1,0:T(8,128)(2,1)S(1)}, bf16[384,384]{1,0:T(8,1...) custom-call(s32[8,256]{1,0:T(8,128)S(1)} %pad_add_fusion.ints, ...), custom_call_target="tpu_custom_call" | custom-call | tf_op jit(solution)/shard_map/front/pallas_call | solution.py:346
  42.5 13.5 %attend.1.packed = bf16[384,1024]{1,0:T(8,128)(2,1)S(1)} custom-call(s32[64,128]{1,0:T(8,128)S(1)} %get-tuple-element.13.bounds, s32[32,128]{1,0:T(8,128)S(1)} %get-tuple-element.14.lanes, bf16[384,1024]{1,0:T(8,128)(2,1)S(1)} %get-tuple-element.15.qsort, bf16[384,384]{1,0:T(8,128)(2,1)S(1)} %get-tuple-element.16.one, ...), custom_call_target="tpu_custom_call" | custom-call | tf_op jit(solution)/shard_map/attend/pallas_call | solution.py:461
  56.0 12.6 %back.1.ret = bf16[384,1024]{1,0:T(8,128)(2,1)S(1)} custom-call(bf16[384,1024]{1,0:T(8,128)(2,1)S(1)} %attend.1.packed), custom_call_target="tpu_custom_call" | custom-call | tf_op jit(solution)/shard_map/back/pallas_call | solution.py:503
  68.6 1.3 %finish.1 = bf16[256,1024]{1,0:T(8,128)(2,1)} custom-call(bf16[384,256]{1,0:T(8,128)(2,1)S(1)} %get-tuple-element.12.pack, bf16[384,1024]{1,0:T(8,128)(2,1)S(1)} %back.1.ret), custom_call_target="tpu_custom_call" | custom-call | tf_op jit(solution)/shard_map/finish/pallas_call | solution.py:520
  (1 shorter events, 0.0 us)
